TPU v7x, 256 devices: a whole 4x4x8 slice. The times are simulated.
256 devices in a mesh: samp: 16 (over y, x_lo, core), var: 16 (over z, x_hi).
Axes of the slice: x: 4 (x_hi: 2, x_lo: 2; x = x_hi * 2 + x_lo), y: 4, z: 8, core: 2. Of those that a mesh axis runs over, the one named last changes fastest.
Arguments:
- dosage: bfloat16 [10752, 8192], P('samp', 'var'), may hold values from 0 to 2
- cohort: int32 [10752], P('samp'), may hold values from 0 to 7, as said below
- live_blocks: int32 [16], P('samp'), may hold values from 1 to 7, as said below
- weight_counts: int32 [8], replicated, may hold values from 50 to 1999
Outputs:
- ld_matrix: float32 [8192, 8192], P('samp', 'var')
Inputs may be any that keep to these rules, and one draw needn't show every extreme that they name: Every cohort has a live sample on every sample-axis device. live_blocks[i] + live_blocks[i + N/2] = 8 for every i below N/2, N the length of live_blocks; some device has 7.
All inputs are finite; a program needn't handle non-finite values.
Results may differ from a plain program's by a relative error of at most 0.0032.
Values may be sent and summed in bfloat16 or wider, within the bound.
A program may use at most 128 MiB of HBM per device.

v0:
```python
import jax
import jax.numpy as jnp
from jax import lax
from jax.sharding import Mesh
from jax.sharding import PartitionSpec as P

COHORTS = 8
BLOCK = 96
HALF = 4
VAR = ("var_0", "var_1")


EPSILON = 1e-05


def passed_along(block, axis, distance):
    devices = range(lax.axis_size(axis))
    route = [((i - distance) % len(devices), i) for i in devices]
    return lax.ppermute(block, axis, route)


def copy_for_each(shard, axis):
    count = lax.axis_size(axis)
    return lax.all_to_all(
        jnp.broadcast_to(shard[None], (count, *shard.shape)), axis, 0, 0, tiled=True
    )


def of_everyone(shard, axis):
    everything = copy_for_each(shard, axis)
    return jnp.sum(everything, axis=0)


def in_one(arrays, axis):
    flat, at, done = (jnp.concatenate([a.reshape(-1) for a in arrays]), 0, [])
    total = of_everyone(flat, axis)
    for a in arrays:
        done.append(total[at : at + a.size].reshape(a.shape))
        at += a.size
    return tuple(done)


def whole_of(shard, axes, dim):
    if not axes:
        return shard
    nearer = lax.all_gather(shard, axes[-1], axis=dim, tiled=True)
    return whole_of(nearer, axes[:-1], dim)


def member_rows(code_rows, weight_row):
    labels = lax.broadcasted_iota(jnp.int32, (COHORTS, code_rows.shape[0]), 0)
    return jnp.where(code_rows[None, :] == labels, weight_row[None, :], 0.0)


def lookup(member, cohort_values):
    return lax.dot_general(
        member,
        cohort_values,
        (((0,), (0,)), ((), ())),
        precision=lax.Precision.HIGHEST,
        preferred_element_type=jnp.float32,
    )


def shards(dosage, cohort, live_blocks, weight_counts):
    own_live = live_blocks[0]
    kept_rows = HALF * BLOCK
    surplus_dose = dosage[kept_rows:]
    surplus_code = cohort[kept_rows:].astype(jnp.bfloat16)
    moved_dose, moved_code = passed_along(
        (surplus_dose, surplus_code), "samp", lax.axis_size("samp") // 2
    )
    offset = own_live * BLOCK
    placed_dose = lax.dynamic_update_slice_in_dim(jnp.zeros_like(dosage), moved_dose, offset, 0)
    placed_code = lax.dynamic_update_slice_in_dim(
        jnp.zeros(cohort.shape, jnp.int32), moved_code.astype(jnp.int32), offset, 0
    )
    row_index = lax.broadcasted_iota(jnp.int32, (kept_rows,), 0)
    from_own = row_index < offset
    dose_rows = jnp.where(from_own[:, None], dosage[:kept_rows], placed_dose[:kept_rows])
    code_rows = jnp.where(from_own, cohort[:kept_rows], placed_code[:kept_rows])
    live_row = jnp.ones((kept_rows,), jnp.float32)
    member = member_rows(code_rows, live_row)
    values = dose_rows.astype(jnp.float32)
    sum_one = jnp.dot(member, values, precision=lax.Precision.HIGHEST)
    sum_two = jnp.dot(member, values * values, precision=lax.Precision.HIGHEST)
    cohort_size = jnp.sum(member, axis=1)
    sum_one, sum_two, cohort_size = in_one((sum_one, sum_two, cohort_size), "samp")
    cohort_mean = sum_one / cohort_size[:, None]
    cohort_var = sum_two / cohort_size[:, None] - cohort_mean * cohort_mean
    inv_spread = lax.rsqrt(cohort_var + EPSILON)
    counts_float = weight_counts.astype(jnp.float32)
    cohort_share = counts_float / jnp.sum(counts_float)
    cohort_scale = jnp.sqrt(cohort_share / cohort_size)
    multiplier = inv_spread * cohort_scale[:, None]
    labels_only = member_rows(code_rows, jnp.ones_like(live_row))
    centered = values - lookup(labels_only, cohort_mean)
    scaled = (live_row[:, None] * centered * lookup(labels_only, multiplier)).astype(jnp.bfloat16)
    panels = whole_of(scaled, VAR, 1)
    return lax.psum_scatter(
        lax.dot_general(
            panels, scaled, (((0,), (0,)), ((), ())), preferred_element_type=jnp.float32
        ),
        "samp",
        scatter_dimension=0,
        tiled=True,
    )


def solution(mesh):
    torus = Mesh(mesh.devices.reshape(mesh.shape["samp"], 8, 2), ("samp", "var_0", "var_1"))
    placed = (P("samp", VAR), P("samp"), P("samp"), P())
    return jax.shard_map(
        shards, mesh=torus, in_specs=placed, out_specs=P("samp", VAR), check_vma=False
    )
```

profile of v0, /device:TPU:8, one launch (start us, length us, event | category | flops | bytes accessed | tf_op | source)
XLA Modules:
  0.0 329.4 jit_solution(8243441042730126214)
XLA Ops:
  6.5 0.0 copy-start
  6.5 0.7 convert.3
  7.2 2.3 collective-permute-start.1
  9.5 1.0 slice.29
  10.5 1.3 collective-permute-start
  12.5 0.0 collective-permute-done.1
  12.5 0.1 convert_dynamic-update-slice_fusion
  12.7 0.7 slice_select_fusion.1
  13.4 0.1 select_reduce_fusion
  13.5 7.1 %collective-permute-done = bf16[288,512]{1,0:T(8,128)(2,1)S(1)} collective-permute-done((bf16[288,512]{1,0:T(8,128)(2,1)S(1)}, bf16[288,512]{1,0:T(8,128)(2,1)S(1)}, u32[]{:S(2)}, u32[]{:S(2)}) %collective-permute-start) | collective-permute-done | bytes 294944 | tf_op jit(solution)/shard_map/ppermute | solution.py:19
  20.7 1.1 slice_select_fusion
  21.8 0.3 convolution_bitcast_fusion.1
  22.1 0.5 convolution_bitcast_fusion
  22.6 1.1 broadcast_in_dim.47
  23.7 4.7 %all-to-all-start = ((f32[16,1,8200]{2,1,0:T(1,128)}), f32[16,1,8200]{2,1,0:T(1,128)S(1)}, u32[]{:S(2)}, u32[]{:S(2)}) async-start(f32[16,1,8200]{2,1,0:T(1,128)} %broadcast_in_dim.47), calls=%async_computation | async-start | bytes 1064960 | tf_op jit(solution)/shard_map/all_to_all | solution.py:24
  28.4 0.0 all-gather.2.cloned.1.call-start
  28.5 1.3 convert_reduce_fusion
  29.8 7.0 %all-to-all-done = f32[16,1,8200]{2,1,0:T(1,128)S(1)} async-done(((f32[16,1,8200]{2,1,0:T(1,128)}), f32[16,1,8200]{2,1,0:T(1,128)S(1)}, u32[]{:S(2)}, u32[]{:S(2)}) %all-to-all-start) | async-done | bytes 524832 | tf_op jit(solution)/shard_map/all_to_all | solution.py:24
  36.8 0.3 reduce_sum.28
  37.1 0.0 copy-done
  37.1 0.6 fusion.39
  37.8 0.8 fusion.2
  38.6 0.9 fusion.1
  39.5 13.4 %all_gather.6 = bf16[384,1024]{1,0:T(8,128)(2,1)} all-gather(bf16[384,512]{1,0:T(8,128)(2,1)S(1)} %fusion.1), channel_id=1, replica_groups=mesh['samp'=16,'var_0'=8,'var_1'=2] {'var_1'}, dimensions={1}, use_global_device_ids=true | all-gather | bytes 1179648 | tf_op jit(solution)/shard_map/all_gather | solution.py:46
  52.9 0.0 all-gather.2.cloned.1.call-update
  53.0 0.0 reduce-scatter.2.cloned.1.call-start
  53.0 77.1 %all-gather.2.cloned.1.call-done = bf16[384,8192]{1,0:T(8,128)(2,1)} async-done(((bf16[384,1024]{1,0:T(8,128)(2,1)}), bf16[384,8192]{1,0:T(8,128)(2,1)}) %all-gather.2.cloned.1.call-update) | async-done | bytes 6291472 | tf_op jit(solution)/shard_map/all_gather | solution.py:46
  130.1 11.1 %fusion.40 = f32[8192,512]{1,0:T(8,128)} fusion(bf16[384,8192]{1,0:T(8,128)(2,1)} %all-gather.2.cloned.1.call-done, bf16[384,512]{1,0:T(8,128)(2,1)S(1)} %fusion.1), kind=kOutput, calls=%fused_computation.55 | convolution fusion | flops 3221225472 | bytes 23461888 | tf_op jit(solution)/shard_map/dot_general | solution.py:101
  141.2 0.0 reduce-scatter.2.cloned.1.call-update
  141.2 181.4 %reduce-scatter.2.cloned.1.call-done = f32[512,512]{1,0:T(8,128)} async-done(((f32[8192,512]{1,0:T(8,128)}), f32[512,512]{1,0:T(8,128)}) %reduce-scatter.2.cloned.1.call-update) | async-done | bytes 1048592 | tf_op jit(solution)/shard_map/reduce_scatter | solution.py:100
  (11 shorter events, 0.1 us)
Async XLA Ops:
  6.5 30.6 %copy-start = (s32[8]{0:T(128)S(1)}, s32[8]{0:T(128)}, u32[]{:S(2)}) copy-start(s32[8]{0:T(128)} %param.7) | copy-start | bytes 100
  7.2 5.3 %collective-permute-start.1 = (bf16[288]{0:T(512)(128)(2,1)S(1)}, bf16[288]{0:T(512)(128)(2,1)S(1)}, u32[]{:S(2)}, u32[]{:S(2)}) collective-permute-start(bf16[288]{0:T(512)(128)(2,1)S(1)} %slice.32), channel_id=1, source_target_pairs={{128,0},{144,16},{160,32},{176,48},{192,64},{208,80},{224,96},{240... | collective-permute-start | bytes 1736 | tf_op jit(solution)/shard_map/ppermute | solution.py:19
  10.5 10.1 %collective-permute-start = (bf16[288,512]{1,0:T(8,128)(2,1)S(1)}, bf16[288,512]{1,0:T(8,128)(2,1)S(1)}, u32[]{:S(2)}, u32[]{:S(2)}) collective-permute-start(bf16[288,512]{1,0:T(8,128)(2,1)S(1)} %slice.29), channel_id=1, source_target_pairs={{128,0},{144,16},{160,32},{176,48},{192,64},{208,80},{224,96},{240... | collective-permute-start | bytes 884744 | tf_op jit(solution)/shard_map/ppermute | solution.py:19
  23.7 13.1 %all-to-all-start = ((f32[16,1,8200]{2,1,0:T(1,128)}), f32[16,1,8200]{2,1,0:T(1,128)S(1)}, u32[]{:S(2)}, u32[]{:S(2)}) async-start(f32[16,1,8200]{2,1,0:T(1,128)} %broadcast_in_dim.47), calls=%async_computation | async-start | bytes 1064960 | tf_op jit(solution)/shard_map/all_to_all | solution.py:24
  28.4 101.7 %all-gather.2.cloned.1.call-start = ((), (), s32[]{:S(2)}) async-start(), calls=%async_computation.2 | async-start | bytes 7077888 | tf_op jit(solution)/shard_map/all_gather | solution.py:46
  53.0 269.6 %reduce-scatter.2.cloned.1.call-start = ((), (), s32[]{:S(2)}) async-start(), calls=%async_computation.3 | async-start | bytes 17825792 | tf_op jit(solution)/shard_map/reduce_scatter | solution.py:100
Sparse Core Ops, SparseCore 0:
  53.1 76.9 all-gather.1
  141.4 181.1 reduce-scatter.1
where the time goes:
time: 332 us; the launch traced here: 329 us
  waiting for transfers between devices  273 us (82%)
  between operations  14.2 us (4%)
  matrix products  13.6 us (4%)
  blocking collectives  13.4 us (4%)
  starting transfers between devices  8.43 us (3%)
  other arithmetic  5.02 us (2%)
    reduce_scatter x1, waiting for transfers between devices, shards(): lax.psum_scatter(lax.dot_general(panels, scaled, (((0,), (0,)), ((), ()))...  181 us
    all_gather x1, waiting for transfers between devices, whole_of(): nearer = lax.all_gather(shard, axes[-1], axis=dim, tiled=True)  77.1 us
    all_gather x1, blocking collectives, whole_of(): nearer = lax.all_gather(shard, axes[-1], axis=dim, tiled=True)  13.4 us
    dot_general x1, matrix products, shards(): lax.dot_general(panels, scaled, (((0,), (0,)), ((), ())), preferred_eleme...  11.1 us
    ppermute x2, waiting for transfers between devices, passed_along(): return lax.ppermute(block, axis, route)  7.12 us
    all_to_all x1, waiting for transfers between devices, copy_for_each(): lax.all_to_all(jnp.broadcast_to(shard[None], (count, *shard.shape)), axis...  6.99 us
  transfers between devices with their start and end apart: 5, of which 4 were waited for; matrix products, arithmetic and copies ran while one was open for 1% of the time, Pallas kernels for 0%

commit v1 on v0

v1 whole, which is shorter than its diff:
```python
import jax
import jax.numpy as jnp
from jax import lax
from jax.experimental import pallas as pl
from jax.experimental.pallas import tpu as pltpu
from jax.sharding import Mesh
from jax.sharding import PartitionSpec as P

COHORTS = 8
BLOCK = 96
HALF = 4
ROWS = HALF * BLOCK
SURPLUS = 3 * BLOCK
LANES = 128
PANEL = 512
DEPTH = 4 * ROWS
EPSILON = 1e-05
MESH = pl.DeviceIdType.MESH
F32 = jnp.float32
BF16 = jnp.bfloat16


def split_three(value):
    first = value.astype(BF16)
    rest = value - first.astype(F32)
    second = rest.astype(BF16)
    third = (rest - second.astype(F32)).astype(BF16)
    return first.astype(F32), second.astype(F32), third.astype(F32)


def kernel(
    dose, labs, live, weights, out,
    own, surplus, surplus_lab, own_lab, cols,
    rows, row_labs, sums, far_sums, panel, turned,
    partial, far_partial, folded, far_folded,
    own_sem, sur_send, sur_recv, slice_send, slice_recv, lab_send, lab_recv,
    sum_send, sum_recv, ring_send, ring_recv, core_send, core_recv,
    z_send, z_recv, part_send, part_recv, fold_send, fold_recv,
):
    y, xl, core, z, xh = (lax.axis_index(a) for a in ("y", "xl", "co", "z", "xh"))
    x = 2 * xh + xl

    def plus(i, d, n):
        return lax.rem(i + d, n)

    def at_x(i, c):
        return {"xh": lax.div(i, 2), "xl": lax.rem(i, 2), "co": c}

    def remote(src, dst, send, recv, device):
        return pltpu.make_async_remote_copy(
            src_ref=src, dst_ref=dst, send_sem=send, recv_sem=recv,
            device_id=device, device_id_type=MESH,
        )

    take_own = pltpu.make_async_copy(dose.at[pl.ds(0, ROWS)], own, own_sem)
    take_own.start()

    barrier = pltpu.get_barrier_semaphore()
    peers = [{"y": plus(y, d, 4)} for d in (1, 2, 3)]
    peers += [{"z": plus(z, d, 8)} for d in (1, 7)]
    peers += [
        at_x(plus(x, d, 4), plus(core, c, 2))
        for d in range(4) for c in range(2) if d or c
    ]
    for peer in peers:
        pl.semaphore_signal(barrier, inc=1, device_id=peer, device_id_type=MESH)
    pl.semaphore_wait(barrier, len(peers))

    opposite = {"y": plus(y, 2, 4)}
    sends = [
        remote(labs.at[1], surplus_lab, sur_send.at[3], sur_recv.at[3], opposite)
    ]
    for b in range(3):
        sends.append(remote(
            dose.at[pl.ds(ROWS + b * BLOCK, BLOCK)], surplus.at[pl.ds(b * BLOCK, BLOCK)],
            sur_send.at[b], sur_recv.at[b], opposite,
        ))
    for copy in sends:
        copy.start()
    take_own.wait()
    count = live[0]
    for copy in sends:
        copy.wait()
    own_lab[...] = jnp.maximum(labs[0], surplus_lab[...])
    for slot in range(HALF):
        block = own[slot * BLOCK : (slot + 1) * BLOCK, :]
        if slot:
            at = (3 - slot) * BLOCK
            other = surplus[at : at + BLOCK, :]
            block = jnp.where(slot < count, block, other)
        for s in range(4):
            cols[s, slot * BLOCK : (slot + 1) * BLOCK, :] = block[:, s * LANES : (s + 1) * LANES]

    mine = 2 * xl + core
    for d in range(4):
        target = plus(x, d, 4)
        device = at_x(target, xh)
        src, dst = cols.at[target], rows.at[mine]
        lab_dst = row_labs.at[mine]
        if d:
            remote(src, dst, slice_send.at[d], slice_recv.at[mine], device).start()
            remote(own_lab, lab_dst, lab_send.at[d], lab_recv.at[mine], device).start()
        else:
            @pl.when(xh != core)
            def _():
                remote(src, dst, slice_send.at[0], slice_recv.at[mine], device).start()
                remote(own_lab, lab_dst, lab_send.at[0], lab_recv.at[mine], device).start()

            @pl.when(xh == core)
            def _():
                pltpu.make_async_copy(src, dst, slice_recv.at[mine]).start()
                pltpu.make_async_copy(own_lab, lab_dst, lab_recv.at[mine]).start()

    cohorts = lax.broadcasted_iota(jnp.int32, (COHORTS, ROWS), 0).astype(F32)

    def one_hot(slot):
        return jnp.where(row_labs[slot] == cohorts, 1.0, 0.0).astype(F32)

    def stacked(hot):
        return jnp.concatenate([hot, hot, hot, jnp.zeros_like(hot)], axis=0).astype(BF16)

    for slot in range(4):
        pltpu.make_async_copy(cols.at[0], rows.at[slot], slice_recv.at[slot]).wait()
        pltpu.make_async_copy(own_lab, row_labs.at[slot], lab_recv.at[slot]).wait()

    total = jnp.zeros((24, LANES), F32)
    for slot in range(4):
        hot = one_hot(slot)
        hots = stacked(hot)
        value = rows[slot]
        wide = value.astype(F32)
        square = wide * wide
        high = square.astype(BF16)
        low = (square - high.astype(F32)).astype(BF16)
        dots = [jnp.dot(hots, v, preferred_element_type=F32)[:COHORTS] for v in (value, high, low)]
        members = jnp.broadcast_to(jnp.sum(hot, axis=1, keepdims=True), (COHORTS, LANES))
        total = total + jnp.concatenate([dots[0], dots[1] + dots[2], members], axis=0)
    sums[...] = total
    sends = [
        remote(sums, far_sums.at[d - 1], sum_send.at[d - 1], sum_recv.at[d - 1], {"y": plus(y, d, 4)})
        for d in (1, 2, 3)
    ]
    for copy in sends:
        copy.start()
    for copy in sends:
        copy.wait()
    total = sums[...] + far_sums[0] + far_sums[1] + far_sums[2]
    size = total[16:24]
    mean = total[0:8] / size
    var = total[8:16] / size - mean * mean + EPSILON
    spread = lax.rsqrt(var)
    spread = spread * (1.5 - 0.5 * var * spread * spread)
    weight = jnp.zeros((COHORTS, LANES), F32)
    all_weights = jnp.float32(0.0)
    labels = lax.broadcasted_iota(jnp.int32, (COHORTS, LANES), 0)
    for c in range(COHORTS):
        w = weights[c].astype(F32)
        all_weights = all_weights + w
        weight = jnp.where(labels == c, w, weight)
    multiplier = spread * jnp.sqrt(weight / all_weights / size)
    table = jnp.concatenate([
        jnp.concatenate(list(split_three(mean)) + [jnp.zeros_like(mean)], axis=0),
        jnp.concatenate(list(split_three(multiplier)) + [jnp.zeros_like(mean)], axis=0),
    ], axis=1).astype(BF16)

    group = 4 * core + x

    def lanes(g):
        return pl.ds(pl.multiple_of(g * LANES, LANES), LANES)

    for slot in range(4):
        hots = stacked(one_hot(slot))
        found = lax.dot_general(hots, table, (((0,), (0,)), ((), ())), preferred_element_type=F32)
        scaled = (rows[slot].astype(F32) - found[:, :LANES]) * found[:, LANES:]
        panel[slot * ROWS : (slot + 1) * ROWS, lanes(group)] = scaled.astype(BF16)
        turned[z, :, slot * ROWS : (slot + 1) * ROWS] = scaled.T.astype(BF16)

    half_lanes = LANES // 2

    def z_copy(step, way):
        d = (9 - step) if way == 0 else (step - 1)
        src = plus(z, d, 8)
        ref = turned.at[src]
        if step == 4:
            ref = turned.at[src, pl.ds(way * half_lanes, half_lanes)]
        return remote(
            ref, ref, z_send.at[way, step - 1], z_recv.at[way, step - 1],
            {"z": plus(z, 1 if way == 0 else 7, 8)},
        )

    def z_wait_recv(step, way):
        z_copy(step, way).wait_recv()

    def ring_copy(which):
        right, left = plus(x, 1, 4), plus(x, 3, 4)
        who = (x, x, left, right)[which]
        ref = panel.at[:, lanes(4 * core + who)]
        if which >= 2:
            half = pl.ds((which - 2) * (DEPTH // 2), DEPTH // 2)
            ref = panel.at[half, lanes(4 * core + who)]
        return remote(
            ref, ref, ring_send.at[which], ring_recv.at[which],
            at_x((right, left, right, left)[which], core),
        )

    def core_copy(d):
        ref = panel.at[:, lanes(4 * core + plus(x, d, 4))]
        return remote(ref, ref, core_send.at[d], core_recv.at[d], {"co": 1 - core})

    z_copy(1, 0).start()
    z_copy(1, 1).start()
    ring_copy(0).start()
    ring_copy(1).start()
    core_copy(0).start()
    ring_copy(0).wait_recv()
    ring_copy(2).start()
    core_copy(3).start()
    ring_copy(1).wait_recv()
    ring_copy(3).start()
    core_copy(1).start()
    z_wait_recv(1, 0)
    z_copy(2, 0).start()
    z_wait_recv(1, 1)
    z_copy(2, 1).start()
    ring_copy(2).wait_recv()
    ring_copy(3).wait_recv()
    core_copy(2).start()
    for d in range(4):
        core_copy(d).wait_recv()

    def part_copy(s):
        owner = lax.div(s, 2)
        slot = lax.rem(y - owner + 3, 4)
        return remote(
            partial.at[s], far_partial.at[slot, lax.rem(s, 2)],
            part_send.at[s], part_recv.at[slot, lax.rem(s, 2)], {"y": owner},
        )

    def make_partial(s):
        left = turned[s]

        def tile(n, carry):
            at = pl.ds(pl.multiple_of(n * 256, 256), 256)
            partial[s, :, at] = jnp.dot(left, panel[:, at], preferred_element_type=F32).astype(BF16)
            return carry

        lax.fori_loop(0, 4, tile, 0)

        @pl.when(lax.div(s, 2) != y)
        def _():
            part_copy(s).start()

    make_partial(z)
    make_partial(plus(z, 7, 8))
    make_partial(plus(z, 1, 8))
    for step in (2, 3, 4):
        for way in (0, 1):
            z_wait_recv(step, way)
            if step < 4:
                z_copy(step + 1, way).start()
        if step < 4:
            make_partial(plus(z, 8 - step, 8))
            make_partial(plus(z, step, 8))
        else:
            make_partial(plus(z, 4, 8))

    def fold_copy(d):
        target = plus(x, d, 4)
        src = folded.at[lax.rem(target, 2), :, pl.ds(pl.multiple_of(lax.div(target, 2) * PANEL, PANEL), PANEL)]
        return remote(src, far_folded.at[d - 1], fold_send.at[d - 1], fold_recv.at[d - 1], at_x(target, core))

    for half in range(2):
        for slot in range(3):
            pltpu.make_async_copy(partial.at[0], far_partial.at[slot, half], part_recv.at[slot, half]).wait()
        added = partial[2 * y + half].astype(F32)
        for slot in range(3):
            added = added + far_partial[slot, half].astype(F32)
        folded[half] = added.astype(BF16)
    for d in (1, 2, 3):
        fold_copy(d).start()

    def put(source, value):
        out[pl.ds(pl.multiple_of(source * LANES, LANES), LANES), :] = value.astype(F32)

    put(x, folded[xl, :, pl.ds(pl.multiple_of(xh * PANEL, PANEL), PANEL)])
    for d in (1, 2, 3):
        fold_copy(d).wait_recv()
        put(plus(x, 4 - d, 4), far_folded[d - 1])

    for d in range(4):
        if d:
            remote(cols.at[0], rows.at[mine], slice_send.at[d], slice_recv.at[mine], at_x(x, core)).wait_send()
            remote(own_lab, row_labs.at[mine], lab_send.at[d], lab_recv.at[mine], at_x(x, core)).wait_send()
        else:
            @pl.when(xh != core)
            def _():
                remote(cols.at[0], rows.at[mine], slice_send.at[0], slice_recv.at[mine], at_x(x, core)).wait_send()
                remote(own_lab, row_labs.at[mine], lab_send.at[0], lab_recv.at[mine], at_x(x, core)).wait_send()
    for d in range(4):
        ring_copy(d).wait_send()
        core_copy(d).wait_send()
        for way in (0, 1):
            z_copy(d + 1, way).wait_send()
    for s in range(8):
        @pl.when(y != s // 2)
        def _():
            part_copy(jnp.int32(s)).wait_send()
    for d in (1, 2, 3):
        fold_copy(d).wait_send()


def shards(dosage, cohort, live_blocks, weight_counts):
    slot = lax.broadcasted_iota(jnp.int32, cohort.shape, 0) // BLOCK
    code = jnp.where(slot < live_blocks[0], cohort, -1).astype(F32).reshape(7, BLOCK)
    none = jnp.full((BLOCK,), -1.0, F32)
    labs = jnp.stack([
        jnp.concatenate([code[0], code[1], code[2], code[3]]),
        jnp.concatenate([none, code[6], code[5], code[4]]),
    ])
    labs = jnp.broadcast_to(labs[:, None, :], (2, COHORTS, ROWS))
    vmem = pl.BlockSpec(memory_space=pltpu.VMEM)
    smem = pl.BlockSpec(memory_space=pltpu.SMEM)
    dma = pltpu.SemaphoreType.DMA
    return pl.pallas_call(
        kernel,
        out_shape=jax.ShapeDtypeStruct((PANEL, PANEL), F32),
        in_specs=[pl.BlockSpec(memory_space=pl.ANY), vmem, smem, smem],
        out_specs=vmem,
        scratch_shapes=[
            pltpu.VMEM((ROWS, PANEL), BF16),
            pltpu.VMEM((SURPLUS, PANEL), BF16),
            pltpu.VMEM((COHORTS, ROWS), F32),
            pltpu.VMEM((COHORTS, ROWS), F32),
            pltpu.VMEM((4, ROWS, LANES), BF16),
            pltpu.VMEM((4, ROWS, LANES), BF16),
            pltpu.VMEM((4, COHORTS, ROWS), F32),
            pltpu.VMEM((24, LANES), F32),
            pltpu.VMEM((3, 24, LANES), F32),
            pltpu.VMEM((DEPTH, 8 * LANES), BF16),
            pltpu.VMEM((8, LANES, DEPTH), BF16),
            pltpu.VMEM((8, LANES, 8 * LANES), BF16),
            pltpu.VMEM((3, 2, LANES, 8 * LANES), BF16),
            pltpu.VMEM((2, LANES, 8 * LANES), BF16),
            pltpu.VMEM((3, LANES, PANEL), BF16),
            dma, dma((4,)), dma((4,)), dma((4,)), dma((4,)), dma((4,)), dma((4,)),
            dma((3,)), dma((3,)), dma((4,)), dma((4,)), dma((4,)), dma((4,)),
            dma((2, 4)), dma((2, 4)), dma((8,)), dma((3, 2)), dma((3,)), dma((3,)),
        ],
        compiler_params=pltpu.CompilerParams(
            collective_id=0, has_side_effects=True, vmem_limit_bytes=60 * 1024 * 1024
        ),
    )(dosage, labs, live_blocks, weight_counts)


def solution(mesh):
    torus = Mesh(mesh.devices.reshape(4, 2, 2, 8, 2), ("y", "xl", "co", "z", "xh"))
    samp, var = ("y", "xl", "co"), ("z", "xh")
    placed = (P(samp, var), P(samp), P(samp), P())
    return jax.shard_map(
        shards, mesh=torus, in_specs=placed, out_specs=P(samp, var), check_vma=False
    )
```

time: 332 us -> 99.1 us (0.30)
  the two profiles are of different devices: /device:TPU:8 before, /device:TPU:48 now
where the time goes in v1:
time: 99.1 us; the launch traced here: 98.9 us
  Pallas kernels  94.5 us (95%)
  local copies, waits for them, and re-layouts  2.97 us (3%)
    pallas_call x1, Pallas kernels, shards(): pl.pallas_call(kernel, out_shape=jax.ShapeDtypeStruct((PANEL, PANEL), F32...  94.5 us
    unnamed x1, local copies, waits for them, and re-layouts  2.26 us

profile of v1, /device:TPU:48, one launch (start us, length us, event | category | flops | bytes accessed | tf_op | source)
XLA Modules:
  0.0 98.9 jit_solution(5250200451690192239)
XLA Ops:
  0.7 0.7 select_convert_fusion
  1.4 0.1 fusion.4
  1.4 0.1 pad_maximum_fusion.1
  1.5 0.6 broadcast_in_dim.12.labs
  2.2 94.5 %shard_map.46 = f32[512,512]{1,0:T(8,128)} custom-call(bf16[672,512]{1,0:T(8,128)(2,1)} %dose.1, f32[2,8,384]{2,1,0:T(8,128)} %broadcast_in_dim.12.labs, s32[1]{0:T(128)} %copy.6.live, s32[8]{0:T(128)} %weights.1), custom_call_target="tpu_custom_call" | custom-call | tf_op jit(solution)/shard_map/pallas_call | solution.py:324
  96.6 2.3 %copy.7 = f32[512,512]{1,0:T(8,128)} copy(f32[512,512]{1,0:T(8,128)} %shard_map.46) | data formatting | bytes 2097152
  (5 shorter events, 0.0 us)

commit v2 on v0

v2 whole, which is shorter than its diff:
```python
import jax
import jax.numpy as jnp
from jax import lax
from jax.experimental import pallas as pl
from jax.experimental.pallas import tpu as pltpu
from jax.sharding import Mesh
from jax.sharding import PartitionSpec as P

COHORTS = 8
BLOCK = 96
HALF = 4
ROWS = HALF * BLOCK
LANES = 128
PANEL = 512
DEPTH = 4 * ROWS
WIDTH = 2 * PANEL
EPSILON = 1e-05
MESH = pl.DeviceIdType.MESH
F32 = jnp.float32
BF16 = jnp.bfloat16


def split_three(value):
    first = value.astype(BF16)
    rest = value - first.astype(F32)
    second = rest.astype(BF16)
    third = (rest - second.astype(F32)).astype(BF16)
    return first.astype(F32), second.astype(F32), third.astype(F32)


def kernel(
    dose, labs, live, weights, out,
    own, relay, surplus, surplus_lab, own_lab, cols,
    raw, row_labs, hot_ref, sums, far_sums, row_tab, z_tab,
    z_raw, panel, turned, keep, partial, mid_in, acc_in, dir_in, folded,
    own_sem, sur_send, sur_recv, rel_send, rel_recv, surlab_send, surlab_recv,
    slice_send, slice_recv, lab_send, lab_recv, sum_send, sum_recv,
    rowtab_send, rowtab_recv, ztab_send, ztab_recv,
    ring_send, ring_recv, fwd_send, fwd_recv, core_send, core_recv,
    z_send, z_recv, part_send, mid_recv, acc_recv, dir_recv, fold_send, fold_recv,
):
    y, xl, core, z, xh = (lax.axis_index(a) for a in ("y", "xl", "co", "z", "xh"))
    x = 2 * xh + xl

    def plus(i, d, n):
        return lax.rem(i + d, n)

    def at_x(i, c):
        return {"xh": lax.div(i, 2), "xl": lax.rem(i, 2), "co": c}

    def remote(src, dst, send, recv, device):
        return pltpu.make_async_remote_copy(
            src_ref=src, dst_ref=dst, send_sem=send, recv_sem=recv,
            device_id=device, device_id_type=MESH,
        )

    take_own = pltpu.make_async_copy(dose.at[pl.ds(0, ROWS)], own, own_sem)
    take_own.start()

    barrier = pltpu.get_barrier_semaphore()
    row_peers = [(d, c) for d in range(4) for c in range(2) if d or c]
    peers = [{"y": plus(y, d, 4)} for d in (1, 2, 3)]
    peers += [{"z": plus(z, d, 8)} for d in range(1, 8)]
    peers += [at_x(plus(x, d, 4), plus(core, c, 2)) for d, c in row_peers]
    for peer in peers:
        pl.semaphore_signal(barrier, inc=1, device_id=peer, device_id_type=MESH)
    pl.semaphore_wait(barrier, len(peers))

    drains = []

    onward = {"y": plus(y, 1 + 2 * core, 4)}
    opposite = {"y": plus(y, 2, 4)}

    def sur_copy(b):
        return remote(
            dose.at[pl.ds((6 - b) * BLOCK, BLOCK)], relay.at[b], sur_send.at[b], sur_recv.at[b], onward
        )

    def rel_copy(b):
        return remote(relay.at[b], surplus.at[b], rel_send.at[b], rel_recv.at[b], onward)

    surlab_copy = remote(labs.at[1], surplus_lab, surlab_send, surlab_recv, opposite)
    for b in range(3):
        sur_copy(b).start()
        drains.append(sur_copy(b))
        drains.append(rel_copy(b))
    surlab_copy.start()
    drains.append(surlab_copy)

    def pass_relay(b):
        sur_copy(b).wait_recv()
        rel_copy(b).start()

    group = 4 * core + x
    mine = 2 * xl + core

    def band(slot):
        return pl.ds(slot * BLOCK, BLOCK)

    def slice_copy(slot, d):
        target = plus(x, d, 4)
        if slot == 0:
            src = own.at[band(0), pl.ds(pl.multiple_of(target * LANES, LANES), LANES)]
        else:
            src = cols.at[target, band(slot)]
        dst = raw.at[4 * xh + target, mine, band(slot)]
        return remote(src, dst, slice_send.at[slot, d], slice_recv.at[slot, mine], at_x(target, xh))

    def slice_local(slot):
        if slot == 0:
            src = own.at[band(0), pl.ds(pl.multiple_of(x * LANES, LANES), LANES)]
        else:
            src = cols.at[x, band(slot)]
        return pltpu.make_async_copy(src, raw.at[group, mine, band(slot)], slice_recv.at[slot, mine])

    def lab_copy(d):
        target = plus(x, d, 4)
        return remote(
            own_lab, row_labs.at[mine], lab_send.at[d], lab_recv.at[mine], at_x(target, xh)
        )

    def send_slices(slot):
        for d in (1, 2, 3):
            slice_copy(slot, d).start()
            drains.append(slice_copy(slot, d))

        @pl.when(xh != core)
        def _():
            slice_copy(slot, 0).start()

        @pl.when(xh == core)
        def _():
            slice_local(slot).start()

    def send_labels():
        surlab_copy.wait_recv()
        own_lab[...] = jnp.maximum(labs[0], surplus_lab[...])
        for d in (1, 2, 3):
            lab_copy(d).start()
            drains.append(lab_copy(d))

        @pl.when(xh != core)
        def _():
            lab_copy(0).start()

        @pl.when(xh == core)
        def _():
            pltpu.make_async_copy(own_lab, row_labs.at[mine], lab_recv.at[mine]).start()

    def fill_slot(slot):
        rel_copy(slot - 1).wait_recv()
        block = jnp.where(slot < live[0], own[slot * BLOCK : (slot + 1) * BLOCK, :], surplus[slot - 1])
        for s in range(4):
            cols[s, slot * BLOCK : (slot + 1) * BLOCK, :] = block[:, s * LANES : (s + 1) * LANES]
        send_slices(slot)

    def z_copy(step, way, slot):
        d = (9 - step) if way == 0 else (step - 1)
        at = plus(z, d, 8)
        dst = z_raw.at[at, :, band(slot)]
        src = raw.at[group, :, band(slot)] if step == 1 else dst
        return remote(
            src, dst, z_send.at[way, step - 1, slot], z_recv.at[way, step - 1, slot],
            {"z": plus(z, 1 if way == 0 else 7, 8)},
        )

    def goes(step, way, slot):
        return step < 4 or (slot < 2) == (way == 0)

    def z_start(step, way, slot):
        if goes(step, way, slot):
            z_copy(step, way, slot).start()
            drains.append(z_copy(step, way, slot))

    def z_pass(step, slot):
        for way in (0, 1):
            if goes(step, way, slot):
                z_copy(step, way, slot).wait_recv()
                if step < 4:
                    z_start(step + 1, way, slot)

    right, left = plus(x, 1, 4), plus(x, 3, 4)

    def ring_copy(way, slot):
        ref = raw.at[group, :, band(slot)]
        return remote(
            ref, ref, ring_send.at[way, slot], ring_recv.at[way, slot],
            at_x(right if way == 0 else left, core),
        )

    def fwd_copy(slot):
        who, to = (left, right) if slot < 2 else (right, left)
        ref = raw.at[4 * core + who, :, band(slot)]
        return remote(ref, ref, fwd_send.at[slot], fwd_recv.at[slot], at_x(to, core))

    def core_copy(d, slot):
        ref = raw.at[4 * core + plus(x, d, 4), :, band(slot)]
        return remote(ref, ref, core_send.at[d, slot], core_recv.at[d, slot], {"co": 1 - core})

    def core_start(d, slot):
        core_copy(d, slot).start()
        drains.append(core_copy(d, slot))

    def send_slot(slot):
        for source in range(4):
            pltpu.make_async_copy(
                cols.at[0, band(slot)], raw.at[group, source, band(slot)], slice_recv.at[slot, source]
            ).wait()
        for way in (0, 1):
            z_start(1, way, slot)
        for way in (0, 1):
            ring_copy(way, slot).start()
            drains.append(ring_copy(way, slot))
        core_start(0, slot)

    def pass_ring(slot):
        ring_copy(0, slot).wait_recv()
        if slot < 2:
            fwd_copy(slot).start()
        core_start(3, slot)
        ring_copy(1, slot).wait_recv()
        if slot >= 2:
            fwd_copy(slot).start()
        core_start(1, slot)
        drains.append(fwd_copy(slot))

    def pass_far(slot):
        fwd_copy(slot).wait_recv()
        core_start(2, slot)

    take_own.wait()
    send_slices(0)
    send_labels()
    pass_relay(0)
    send_slot(0)
    pass_relay(1)
    fill_slot(1)
    pass_relay(2)
    z_pass(1, 0)
    pass_ring(0)
    fill_slot(2)
    send_slot(1)
    fill_slot(3)
    send_slot(2)
    z_pass(2, 0)
    z_pass(1, 1)
    pass_ring(1)
    pass_far(0)
    send_slot(3)

    for source in range(4):
        pltpu.make_async_copy(own_lab, row_labs.at[source], lab_recv.at[source]).wait()
    cohorts = lax.broadcasted_iota(jnp.int32, (COHORTS, ROWS), 0).astype(F32)
    total = jnp.zeros((24, LANES), F32)
    for source in range(4):
        hot = jnp.where(row_labs[source] == cohorts, 1.0, 0.0).astype(F32)
        hots = jnp.concatenate([hot, hot, hot, jnp.zeros_like(hot)], axis=0).astype(BF16)
        hot_ref[source] = hots
        value = raw[group, source]
        wide = value.astype(F32)
        square = wide * wide
        high = square.astype(BF16)
        low = (square - high.astype(F32)).astype(BF16)
        dots = [jnp.dot(hots, v, preferred_element_type=F32)[:COHORTS] for v in (value, high, low)]
        members = jnp.broadcast_to(jnp.sum(hot, axis=1, keepdims=True), (COHORTS, LANES))
        total = total + jnp.concatenate([dots[0], dots[1] + dots[2], members], axis=0)
    sums[...] = total
    sum_copies = [
        remote(sums, far_sums.at[d - 1], sum_send.at[d - 1], sum_recv.at[d - 1], {"y": plus(y, d, 4)})
        for d in (1, 2, 3)
    ]
    for copy in sum_copies:
        copy.start()
        drains.append(copy)

    z_pass(1, 2)
    pass_ring(2)
    pass_far(1)

    for copy in sum_copies:
        copy.wait_recv()
    total = sums[...] + far_sums[0] + far_sums[1] + far_sums[2]
    size = total[16:24]
    mean = total[0:8] / size
    var = total[8:16] / size - mean * mean + EPSILON
    spread = lax.rsqrt(var)
    spread = spread * (1.5 - 0.5 * var * spread * spread)
    weight = jnp.zeros((COHORTS, LANES), F32)
    all_weights = jnp.float32(0.0)
    labels = lax.broadcasted_iota(jnp.int32, (COHORTS, LANES), 0)
    for c in range(COHORTS):
        w = weights[c].astype(F32)
        all_weights = all_weights + w
        weight = jnp.where(labels == c, w, weight)
    multiplier = spread * jnp.sqrt(weight / all_weights / size)
    row_tab[group] = jnp.concatenate([mean, multiplier], axis=0)

    def rowtab_copy(d, c):
        ref = row_tab.at[group]
        return remote(
            ref, ref, rowtab_send.at[2 * d + c], rowtab_recv.at[2 * d + c],
            at_x(plus(x, d, 4), plus(core, c, 2)),
        )

    def ztab_copy(d):
        return remote(
            row_tab.at[group], z_tab.at[z], ztab_send.at[d - 1], ztab_recv.at[d - 1], {"z": plus(z, d, 8)}
        )

    for d, c in row_peers:
        rowtab_copy(d, c).start()
        drains.append(rowtab_copy(d, c))
    for d in (1, 7, 2, 6, 3, 5, 4):
        ztab_copy(d).start()
        drains.append(ztab_copy(d))

    z_pass(2, 1)
    z_pass(1, 3)
    pass_ring(3)
    for slot in (2, 3):
        pass_far(slot)
    z_pass(3, 0)

    def packed(both):
        mean, multiplier = both[:COHORTS], both[COHORTS:]
        none = jnp.zeros_like(mean)
        return jnp.concatenate([
            jnp.concatenate(list(split_three(mean)) + [none], axis=0),
            jnp.concatenate(list(split_three(multiplier)) + [none], axis=0),
        ], axis=1).astype(BF16)

    def scaled(value, source, table):
        found = lax.dot_general(
            hot_ref[source], table, (((0,), (0,)), ((), ())), preferred_element_type=F32
        )
        return (value.astype(F32) - found[:, :LANES]) * found[:, LANES:]

    for d, c in row_peers:
        rowtab_copy(d, c).wait_recv()
    for d in range(4):
        for slot in range(4):
            core_copy(d, slot).wait_recv()
    z_pass(2, 2)

    def fill_panel(g, carry):
        table = packed(row_tab[g])
        at = pl.ds(pl.multiple_of(g * LANES, LANES), LANES)
        for source in range(4):
            value = scaled(raw[g, source], source, table)
            panel[source * ROWS : (source + 1) * ROWS, at] = value.astype(BF16)
        return carry

    lax.fori_loop(0, 8, fill_panel, 0)

    sign = 1 - 2 * core

    def hops_to(s):
        return lax.rem(sign * (lax.div(s, 2) - y) + 4, 4)

    def half_of(ref, h):
        return ref.at[:, pl.ds(h * PANEL, PANEL)]

    def part_copy(s, h, kind):
        p = lax.rem(s, 2)
        dst, recv, device = {
            "mid": (mid_in.at[p, h], mid_recv.at[p, h], onward),
            "acc": (acc_in.at[p, h], acc_recv.at[p, h], onward),
            "dir": (dir_in.at[p, h], dir_recv.at[p, h], {"y": plus(y, 3 - 2 * core, 4)}),
        }[kind]
        return remote(half_of(partial.at[s], h), dst, part_send.at[s, h], recv, device)

    def make_partial(s, value_of, table):
        table = packed(table)
        for source in range(4):
            value = scaled(value_of(source), source, table)
            turned[:, source * ROWS : (source + 1) * ROWS] = value.T.astype(BF16)
        hops = hops_to(s)
        for h in range(2):
            def tile(n, carry):
                at = pl.ds(pl.multiple_of(h * PANEL + n * 256, 256), 256)
                value = jnp.dot(turned[...], panel[:, at], preferred_element_type=F32)
                keep[s, :, at] = value
                partial[s, :, at] = value.astype(BF16)
                return carry

            lax.fori_loop(0, 2, tile, 0)

            @pl.when(hops == 2)
            def _():
                part_copy(s, h, "mid").start()

            @pl.when(hops == 3)
            def _():
                part_copy(s, h, "dir").start()

    def add_relay(s):
        @pl.when(hops_to(s) == 1)
        def _():
            for h in range(2):
                p = lax.rem(s, 2)
                part_copy(s, h, "mid").wait_recv()
                at = slice(h * PANEL, (h + 1) * PANEL)
                partial[s, :, at] = (keep[s, :, at] + mid_in[p, h].astype(F32)).astype(BF16)
                part_copy(s, h, "acc").start()

    def from_z(d):
        s = plus(z, d, 8)
        ztab_copy(8 - d).wait_recv()
        make_partial(s, lambda source: z_raw[s, source], z_tab[s])

    make_partial(z, lambda source: raw[group, source], row_tab[group])
    z_pass(2, 3)
    z_pass(3, 1)
    from_z(7)
    from_z(1)
    add_relay(z)
    z_pass(3, 2)
    z_pass(3, 3)
    from_z(6)
    add_relay(plus(z, 7, 8))
    from_z(2)
    add_relay(plus(z, 1, 8))
    from_z(5)
    add_relay(plus(z, 6, 8))
    from_z(3)
    add_relay(plus(z, 2, 8))
    add_relay(plus(z, 5, 8))
    for slot in range(4):
        z_pass(4, slot)
    from_z(4)
    add_relay(plus(z, 3, 8))
    add_relay(plus(z, 4, 8))

    def fold_copy(p, h):
        target = 2 * h + p
        d = plus(target, 4 - x, 4) - 1
        return remote(
            folded.at[p, h], out.at[pl.ds(pl.multiple_of(x * LANES, LANES), LANES)],
            fold_send.at[p, h], fold_recv.at[d], at_x(target, core),
        )

    for p in (plus(z, 1, 2), plus(z, 0, 2)):
        for h in range(2):
            s = 2 * y + p
            part_copy(s, h, "acc").wait_recv()
            part_copy(s, h, "dir").wait_recv()
            at = slice(h * PANEL, (h + 1) * PANEL)
            value = keep[s, :, at] + acc_in[p, h].astype(F32) + dir_in[p, h].astype(F32)
            value = value.astype(BF16)

            @pl.when(2 * h + p != x)
            def _():
                folded[p, h] = value
                fold_copy(p, h).start()

            @pl.when(2 * h + p == x)
            def _():
                out[pl.ds(pl.multiple_of(x * LANES, LANES), LANES), :] = value

    for d in (1, 2, 3):
        pltpu.make_async_copy(
            folded.at[0, 0], out.at[pl.ds(0, LANES)], fold_recv.at[d - 1]
        ).wait()

    for copy in drains:
        copy.wait_send()

    @pl.when(xh != core)
    def _():
        for slot in range(4):
            slice_copy(slot, 0).wait_send()
        lab_copy(0).wait_send()

    for s in range(8):
        @pl.when(y != s // 2)
        def _():
            for h in range(2):
                part_copy(jnp.int32(s), h, "dir").wait_send()

    for p in range(2):
        for h in range(2):
            @pl.when(2 * h + p != x)
            def _():
                fold_copy(p, h).wait_send()


def shards(dosage, cohort, live_blocks, weight_counts):
    slot = lax.broadcasted_iota(jnp.int32, cohort.shape, 0) // BLOCK
    code = jnp.where(slot < live_blocks[0], cohort, -1).astype(F32).reshape(7, BLOCK)
    none = jnp.full((BLOCK,), -1.0, F32)
    labs = jnp.stack([
        jnp.concatenate([code[0], code[1], code[2], code[3]]),
        jnp.concatenate([none, code[6], code[5], code[4]]),
    ])
    labs = jnp.broadcast_to(labs[:, None, :], (2, COHORTS, ROWS))
    vmem = pl.BlockSpec(memory_space=pltpu.VMEM)
    smem = pl.BlockSpec(memory_space=pltpu.SMEM)

    def dma(*shape):
        return pltpu.SemaphoreType.DMA(shape)

    ld = pl.pallas_call(
        kernel,
        out_shape=jax.ShapeDtypeStruct((PANEL, PANEL), BF16),
        in_specs=[pl.BlockSpec(memory_space=pl.ANY), vmem, smem, smem],
        out_specs=vmem,
        scratch_shapes=[
            pltpu.VMEM((ROWS, PANEL), BF16),
            pltpu.VMEM((3, BLOCK, PANEL), BF16),
            pltpu.VMEM((3, BLOCK, PANEL), BF16),
            pltpu.VMEM((COHORTS, ROWS), F32),
            pltpu.VMEM((COHORTS, ROWS), F32),
            pltpu.VMEM((4, ROWS, LANES), BF16),
            pltpu.VMEM((8, 4, ROWS, LANES), BF16),
            pltpu.VMEM((4, COHORTS, ROWS), F32),
            pltpu.VMEM((4, 32, ROWS), BF16),
            pltpu.VMEM((24, LANES), F32),
            pltpu.VMEM((3, 24, LANES), F32),
            pltpu.VMEM((8, 16, LANES), F32),
            pltpu.VMEM((8, 16, LANES), F32),
            pltpu.VMEM((8, 4, ROWS, LANES), BF16),
            pltpu.VMEM((DEPTH, WIDTH), BF16),
            pltpu.VMEM((LANES, DEPTH), BF16),
            pltpu.VMEM((8, LANES, WIDTH), F32),
            pltpu.VMEM((8, LANES, WIDTH), BF16),
            pltpu.VMEM((2, 2, LANES, PANEL), BF16),
            pltpu.VMEM((2, 2, LANES, PANEL), BF16),
            pltpu.VMEM((2, 2, LANES, PANEL), BF16),
            pltpu.VMEM((2, 2, LANES, PANEL), BF16),
            pltpu.SemaphoreType.DMA, dma(3), dma(3), dma(3), dma(3),
            pltpu.SemaphoreType.DMA, pltpu.SemaphoreType.DMA,
            dma(4, 4), dma(4, 4), dma(4), dma(4), dma(3), dma(3),
            dma(8), dma(8), dma(7), dma(7),
            dma(2, 4), dma(2, 4), dma(4), dma(4), dma(4, 4), dma(4, 4),
            dma(2, 4, 4), dma(2, 4, 4), dma(8, 2), dma(2, 2), dma(2, 2), dma(2, 2),
            dma(2, 2), dma(3),
        ],
        compiler_params=pltpu.CompilerParams(
            collective_id=0, has_side_effects=True, vmem_limit_bytes=60 * 1024 * 1024
        ),
    )(dosage, labs, live_blocks, weight_counts)
    return ld.astype(F32)


def solution(mesh):
    torus = Mesh(mesh.devices.reshape(4, 2, 2, 8, 2), ("y", "xl", "co", "z", "xh"))
    samp, var = ("y", "xl", "co"), ("z", "xh")
    placed = (P(samp, var), P(samp), P(samp), P())
    return jax.shard_map(
        shards, mesh=torus, in_specs=placed, out_specs=P(samp, var), check_vma=False
    )
```

time: 332 us -> 89.1 us (0.27)
  waiting for transfers between devices: 273 us -> 0 us
  Pallas kernels: 0 us -> 84.5 us
  matrix products: 13.6 us -> 0 us
  between operations: 14.2 us -> 0.67 us
  blocking collectives: 13.4 us -> 0 us
  starting transfers between devices: 8.43 us -> 0 us
    reduce_scatter x1 -> x0, waiting for transfers between devices: 181 us -> none  [shards(): lax.psum_scatter(lax.dot_general(panels, scaled, (((0,), (0,)), ((), ()))...]
    pallas_call x0 -> x1, Pallas kernels: none -> 84.5 us  [shards(): pl.pallas_call(kernel, out_shape=jax.ShapeDtypeStruct((PANEL, PANEL), BF1...]
    all_gather x1 -> x0, waiting for transfers between devices: 77.1 us -> none  [whole_of(): nearer = lax.all_gather(shard, axes[-1], axis=dim, tiled=True)]
    dot_general x5 -> x0, matrix products: 13.6 us -> none  [the longest x1 11.1 us: shards(): lax.dot_general(panels, scaled, (((0,), (0,)), ((), ())), preferred_eleme...]
    all_gather x1 -> x0, blocking collectives: 13.4 us -> none  [whole_of(): nearer = lax.all_gather(shard, axes[-1], axis=dim, tiled=True)]
    ppermute x2 -> x0, waiting for transfers between devices: 7.12 us -> none  [passed_along(): return lax.ppermute(block, axis, route)]
    all_to_all x1 -> x0, waiting for transfers between devices: 6.99 us -> none  [copy_for_each(): lax.all_to_all(jnp.broadcast_to(shard[None], (count, *shard.shape)), axis...]
    all_to_all x1 -> x0, starting transfers between devices: 4.73 us -> none  [copy_for_each(): lax.all_to_all(jnp.broadcast_to(shard[None], (count, *shard.shape)), axis...]
  transfers between devices with their start and end apart: 5 -> 0, of which waited for: 4 -> 0; matrix products, arithmetic and copies ran while one was open for 1% -> 0% of each run, Pallas kernels for 0% -> 0%
where the time goes in v2:
time: 89.1 us; the launch traced here: 88.9 us
  Pallas kernels  84.5 us (95%)
  other arithmetic  2.94 us (3%)
    pallas_call x1, Pallas kernels, shards(): pl.pallas_call(kernel, out_shape=jax.ShapeDtypeStruct((PANEL, PANEL), BF1...  84.5 us
    convert_element_type x1, other arithmetic, shards(): return ld.astype(F32)  2.15 us

profile of v2, /device:TPU:8, one launch (start us, length us, event | category | flops | bytes accessed | tf_op | source)
XLA Modules:
  0.0 88.9 jit_solution(2729621148488675724)
XLA Ops:
  0.7 0.7 select_convert_fusion
  1.4 0.1 fusion.4
  1.4 0.1 pad_maximum_fusion.1
  1.5 0.6 broadcast_in_dim.12.labs
  2.2 84.5 %shard_map.46 = bf16[512,512]{1,0:T(8,128)(2,1)} custom-call(bf16[672,512]{1,0:T(8,128)(2,1)} %dose.1, f32[2,8,384]{2,1,0:T(8,128)} %broadcast_in_dim.12.labs, s32[1]{0:T(128)} %copy.5.live, s32[8]{0:T(128)} %weights.1), custom_call_target="tpu_custom_call" | custom-call | tf_op jit(solution)/shard_map/pallas_call | solution.py:502
  86.7 2.1 %convert_element_type.7 = f32[512,512]{1,0:T(8,128)} convert(bf16[512,512]{1,0:T(8,128)(2,1)} %shard_map.46) | non-fusion elementwise | flops 262144 | bytes 1572864 | tf_op jit(solution)/shard_map/convert_element_type | solution.py:542
  (5 shorter events, 0.0 us)

commit v3 on v2

--- a/solution.py
+++ b/solution.py
@@ -9,6 +9,7 @@
 COHORTS = 8
 BLOCK = 96
 HALF = 4
+SURPLUS = 3 * BLOCK
 ROWS = HALF * BLOCK
 LANES = 128
 PANEL = 512
@@ -30,11 +31,11 @@
 
 def kernel(
     dose, labs, live, weights, out,
-    own, relay, surplus, surplus_lab, own_lab, cols,
-    raw, row_labs, hot_ref, sums, far_sums, row_tab, z_tab,
+    own, surplus, surplus_lab, own_lab, cols,
+    raw, row_labs, hot_ref, slice_sums, row_sums, sums, far_sums, row_tab, z_tab,
     z_raw, panel, turned, keep, partial, mid_in, acc_in, dir_in, folded,
-    own_sem, sur_send, sur_recv, rel_send, rel_recv, surlab_send, surlab_recv,
-    slice_send, slice_recv, lab_send, lab_recv, sum_send, sum_recv,
+    own_sem, sur_send, sur_recv, surlab_send, surlab_recv,
+    slice_send, slice_recv, lab_send, lab_recv, rowsum_send, rowsum_recv, sum_send, sum_recv,
     rowtab_send, rowtab_recv, ztab_send, ztab_recv,
     ring_send, ring_recv, fwd_send, fwd_recv, core_send, core_recv,
     z_send, z_recv, part_send, mid_recv, acc_recv, dir_recv, fold_send, fold_recv,
@@ -54,42 +55,55 @@
             device_id=device, device_id_type=MESH,
         )
 
-    take_own = pltpu.make_async_copy(dose.at[pl.ds(0, ROWS)], own, own_sem)
+    take_own = pltpu.make_async_copy(dose, own, own_sem)
     take_own.start()
 
     barrier = pltpu.get_barrier_semaphore()
     row_peers = [(d, c) for d in range(4) for c in range(2) if d or c]
     peers = [{"y": plus(y, d, 4)} for d in (1, 2, 3)]
-    peers += [{"z": plus(z, d, 8)} for d in range(1, 8)]
+    peers += [{"z": plus(z, d, 8)} for d in (1, 7)]
     peers += [at_x(plus(x, d, 4), plus(core, c, 2)) for d, c in row_peers]
     for peer in peers:
         pl.semaphore_signal(barrier, inc=1, device_id=peer, device_id_type=MESH)
+
+    take_own.wait()
+    cohorts = lax.broadcasted_iota(jnp.int32, (COHORTS, ROWS), 0).astype(F32)
+    totals = None
+    for first, count, labels in ((0, ROWS, labs[0]), (ROWS, SURPLUS, labs[2])):
+        hot = jnp.where(labels == cohorts, 1.0, 0.0).astype(F32)[:, :count]
+        hots = jnp.concatenate([hot, hot], axis=0).astype(BF16)
+        value = own[first : first + count, :]
+        wide = value.astype(F32)
+        square = wide * wide
+        high = square.astype(BF16)
+        low = (square - high.astype(F32)).astype(BF16)
+        dots = [jnp.dot(hots, v, preferred_element_type=F32)[:COHORTS] for v in (value, high, low)]
+        members = jnp.broadcast_to(jnp.sum(hot, axis=1, keepdims=True), (COHORTS, PANEL))
+        part = jnp.concatenate([dots[0], dots[1] + dots[2], members], axis=0)
+        totals = part if totals is None else totals + part
+    for s in range(4):
+        slice_sums[s] = totals[:, s * LANES : (s + 1) * LANES]
     pl.semaphore_wait(barrier, len(peers))
 
     drains = []
 
+    opposite = {"y": plus(y, 2, 4)}
     onward = {"y": plus(y, 1 + 2 * core, 4)}
-    opposite = {"y": plus(y, 2, 4)}
 
     def sur_copy(b):
         return remote(
-            dose.at[pl.ds((6 - b) * BLOCK, BLOCK)], relay.at[b], sur_send.at[b], sur_recv.at[b], onward
-        )
-
-    def rel_copy(b):
-        return remote(relay.at[b], surplus.at[b], rel_send.at[b], rel_recv.at[b], onward)
+            dose.at[pl.ds((6 - b) * BLOCK, BLOCK)], surplus.at[b], sur_send.at[b], sur_recv.at[b], opposite
+        )
 
     surlab_copy = remote(labs.at[1], surplus_lab, surlab_send, surlab_recv, opposite)
-    for b in range(3):
-        sur_copy(b).start()
-        drains.append(sur_copy(b))
-        drains.append(rel_copy(b))
-    surlab_copy.start()
-    drains.append(surlab_copy)
-
-    def pass_relay(b):
-        sur_copy(b).wait_recv()
-        rel_copy(b).start()
+
+    def send_surplus():
+        for b in range(3):
+            sur_copy(b).start()
+            drains.append(sur_copy(b))
+            if b == 0:
+                surlab_copy.start()
+                drains.append(surlab_copy)
 
     group = 4 * core + x
     mine = 2 * xl + core
@@ -119,6 +133,25 @@
             own_lab, row_labs.at[mine], lab_send.at[d], lab_recv.at[mine], at_x(target, xh)
         )
 
+    def rowsum_copy(d):
+        target = plus(x, d, 4)
+        return remote(
+            slice_sums.at[target], row_sums.at[mine], rowsum_send.at[d], rowsum_recv.at[mine], at_x(target, xh)
+        )
+
+    def send_row_sums():
+        for d in (1, 2, 3):
+            rowsum_copy(d).start()
+            drains.append(rowsum_copy(d))
+
+        @pl.when(xh != core)
+        def _():
+            rowsum_copy(0).start()
+
+        @pl.when(xh == core)
+        def _():
+            pltpu.make_async_copy(slice_sums.at[x], row_sums.at[mine], rowsum_recv.at[mine]).start()
+
     def send_slices(slot):
         for d in (1, 2, 3):
             slice_copy(slot, d).start()
@@ -148,7 +181,7 @@
             pltpu.make_async_copy(own_lab, row_labs.at[mine], lab_recv.at[mine]).start()
 
     def fill_slot(slot):
-        rel_copy(slot - 1).wait_recv()
+        sur_copy(slot - 1).wait_recv()
         block = jnp.where(slot < live[0], own[slot * BLOCK : (slot + 1) * BLOCK, :], surplus[slot - 1])
         for s in range(4):
             cols[s, slot * BLOCK : (slot + 1) * BLOCK, :] = block[:, s * LANES : (s + 1) * LANES]
@@ -228,54 +261,23 @@
         fwd_copy(slot).wait_recv()
         core_start(2, slot)
 
-    take_own.wait()
-    send_slices(0)
-    send_labels()
-    pass_relay(0)
-    send_slot(0)
-    pass_relay(1)
-    fill_slot(1)
-    pass_relay(2)
-    z_pass(1, 0)
-    pass_ring(0)
-    fill_slot(2)
-    send_slot(1)
-    fill_slot(3)
-    send_slot(2)
-    z_pass(2, 0)
-    z_pass(1, 1)
-    pass_ring(1)
-    pass_far(0)
-    send_slot(3)
-
-    for source in range(4):
-        pltpu.make_async_copy(own_lab, row_labs.at[source], lab_recv.at[source]).wait()
-    cohorts = lax.broadcasted_iota(jnp.int32, (COHORTS, ROWS), 0).astype(F32)
-    total = jnp.zeros((24, LANES), F32)
-    for source in range(4):
-        hot = jnp.where(row_labs[source] == cohorts, 1.0, 0.0).astype(F32)
-        hots = jnp.concatenate([hot, hot, hot, jnp.zeros_like(hot)], axis=0).astype(BF16)
-        hot_ref[source] = hots
-        value = raw[group, source]
-        wide = value.astype(F32)
-        square = wide * wide
-        high = square.astype(BF16)
-        low = (square - high.astype(F32)).astype(BF16)
-        dots = [jnp.dot(hots, v, preferred_element_type=F32)[:COHORTS] for v in (value, high, low)]
-        members = jnp.broadcast_to(jnp.sum(hot, axis=1, keepdims=True), (COHORTS, LANES))
-        total = total + jnp.concatenate([dots[0], dots[1] + dots[2], members], axis=0)
-    sums[...] = total
     sum_copies = [
         remote(sums, far_sums.at[d - 1], sum_send.at[d - 1], sum_recv.at[d - 1], {"y": plus(y, d, 4)})
         for d in (1, 2, 3)
     ]
+
+    send_slices(0)
+    send_row_sums()
+    send_surplus()
+    for source in range(4):
+        pltpu.make_async_copy(slice_sums.at[0], row_sums.at[source], rowsum_recv.at[source]).wait()
+    sums[...] = row_sums[0] + row_sums[1] + row_sums[2] + row_sums[3]
     for copy in sum_copies:
         copy.start()
         drains.append(copy)
-
-    z_pass(1, 2)
-    pass_ring(2)
-    pass_far(1)
+    send_slot(0)
+    send_labels()
+    fill_slot(1)
 
     for copy in sum_copies:
         copy.wait_recv()
@@ -302,24 +304,61 @@
             at_x(plus(x, d, 4), plus(core, c, 2)),
         )
 
-    def ztab_copy(d):
-        return remote(
-            row_tab.at[group], z_tab.at[z], ztab_send.at[d - 1], ztab_recv.at[d - 1], {"z": plus(z, d, 8)}
-        )
+    def ztab_copy(step, way):
+        at = plus(z, (9 - step) if way == 0 else (step - 1), 8)
+        src = row_tab.at[group] if step == 1 else z_tab.at[at]
+        return remote(
+            src, z_tab.at[at], ztab_send.at[way, step - 1], ztab_recv.at[way, step - 1],
+            {"z": plus(z, 1 if way == 0 else 7, 8)},
+        )
+
+    def ztab_start(step, way):
+        if step < 4 or way == 0:
+            ztab_copy(step, way).start()
+            drains.append(ztab_copy(step, way))
+
+    def ztab_pass(step):
+        for way in (0, 1):
+            if step < 4 or way == 0:
+                ztab_copy(step, way).wait_recv()
+                if step < 4:
+                    ztab_start(step + 1, way)
 
     for d, c in row_peers:
         rowtab_copy(d, c).start()
         drains.append(rowtab_copy(d, c))
-    for d in (1, 7, 2, 6, 3, 5, 4):
-        ztab_copy(d).start()
-        drains.append(ztab_copy(d))
-
+    for way in (0, 1):
+        ztab_start(1, way)
+
+    pass_ring(0)
+    z_pass(1, 0)
+    fill_slot(2)
+    send_slot(1)
+    ztab_pass(1)
+    fill_slot(3)
+    send_slot(2)
+    z_pass(2, 0)
+    pass_ring(1)
+    z_pass(1, 1)
+    pass_far(0)
+    send_slot(3)
+    for source in range(4):
+        pltpu.make_async_copy(own_lab, row_labs.at[source], lab_recv.at[source]).wait()
+    for source in range(4):
+        hot = jnp.where(row_labs[source] == cohorts, 1.0, 0.0).astype(F32)
+        hots = jnp.concatenate([hot, hot, hot, jnp.zeros_like(hot)], axis=0)
+        hot_ref[source] = hots.T.astype(BF16)
+    ztab_pass(2)
+    z_pass(1, 2)
+    pass_ring(2)
+    pass_far(1)
     z_pass(2, 1)
+    z_pass(3, 0)
     z_pass(1, 3)
     pass_ring(3)
+    ztab_pass(3)
     for slot in (2, 3):
         pass_far(slot)
-    z_pass(3, 0)
 
     def packed(both):
         mean, multiplier = both[:COHORTS], both[COHORTS:]
@@ -330,9 +369,7 @@
         ], axis=1).astype(BF16)
 
     def scaled(value, source, table):
-        found = lax.dot_general(
-            hot_ref[source], table, (((0,), (0,)), ((), ())), preferred_element_type=F32
-        )
+        found = jnp.dot(hot_ref[source], table, preferred_element_type=F32)
         return (value.astype(F32) - found[:, :LANES]) * found[:, LANES:]
 
     for d, c in row_peers:
@@ -376,14 +413,10 @@
             turned[:, source * ROWS : (source + 1) * ROWS] = value.T.astype(BF16)
         hops = hops_to(s)
         for h in range(2):
-            def tile(n, carry):
-                at = pl.ds(pl.multiple_of(h * PANEL + n * 256, 256), 256)
-                value = jnp.dot(turned[...], panel[:, at], preferred_element_type=F32)
-                keep[s, :, at] = value
-                partial[s, :, at] = value.astype(BF16)
-                return carry
-
-            lax.fori_loop(0, 2, tile, 0)
+            at = slice(h * PANEL, (h + 1) * PANEL)
+            value = jnp.dot(turned[...], panel[:, at], preferred_element_type=F32)
+            keep[s, :, at] = value
+            partial[s, :, at] = value.astype(BF16)
 
             @pl.when(hops == 2)
             def _():
@@ -405,7 +438,6 @@
 
     def from_z(d):
         s = plus(z, d, 8)
-        ztab_copy(8 - d).wait_recv()
         make_partial(s, lambda source: z_raw[s, source], z_tab[s])
 
     make_partial(z, lambda source: raw[group, source], row_tab[group])
@@ -427,6 +459,7 @@
     add_relay(plus(z, 5, 8))
     for slot in range(4):
         z_pass(4, slot)
+    ztab_pass(4)
     from_z(4)
     add_relay(plus(z, 3, 8))
     add_relay(plus(z, 4, 8))
@@ -470,6 +503,7 @@
         for slot in range(4):
             slice_copy(slot, 0).wait_send()
         lab_copy(0).wait_send()
+        rowsum_copy(0).wait_send()
 
     for s in range(8):
         @pl.when(y != s // 2)
@@ -491,8 +525,9 @@
     labs = jnp.stack([
         jnp.concatenate([code[0], code[1], code[2], code[3]]),
         jnp.concatenate([none, code[6], code[5], code[4]]),
+        jnp.concatenate([code[4], code[5], code[6], none]),
     ])
-    labs = jnp.broadcast_to(labs[:, None, :], (2, COHORTS, ROWS))
+    labs = jnp.broadcast_to(labs[:, None, :], (3, COHORTS, ROWS))
     vmem = pl.BlockSpec(memory_space=pltpu.VMEM)
     smem = pl.BlockSpec(memory_space=pltpu.SMEM)
 
@@ -505,15 +540,16 @@
         in_specs=[pl.BlockSpec(memory_space=pl.ANY), vmem, smem, smem],
         out_specs=vmem,
         scratch_shapes=[
-            pltpu.VMEM((ROWS, PANEL), BF16),
-            pltpu.VMEM((3, BLOCK, PANEL), BF16),
+            pltpu.VMEM((ROWS + SURPLUS, PANEL), BF16),
             pltpu.VMEM((3, BLOCK, PANEL), BF16),
             pltpu.VMEM((COHORTS, ROWS), F32),
             pltpu.VMEM((COHORTS, ROWS), F32),
             pltpu.VMEM((4, ROWS, LANES), BF16),
             pltpu.VMEM((8, 4, ROWS, LANES), BF16),
             pltpu.VMEM((4, COHORTS, ROWS), F32),
-            pltpu.VMEM((4, 32, ROWS), BF16),
+            pltpu.VMEM((4, ROWS, 32), BF16),
+            pltpu.VMEM((4, 24, LANES), F32),
+            pltpu.VMEM((4, 24, LANES), F32),
             pltpu.VMEM((24, LANES), F32),
             pltpu.VMEM((3, 24, LANES), F32),
             pltpu.VMEM((8, 16, LANES), F32),
@@ -527,10 +563,10 @@
             pltpu.VMEM((2, 2, LANES, PANEL), BF16),
             pltpu.VMEM((2, 2, LANES, PANEL), BF16),
             pltpu.VMEM((2, 2, LANES, PANEL), BF16),
-            pltpu.SemaphoreType.DMA, dma(3), dma(3), dma(3), dma(3),
+            pltpu.SemaphoreType.DMA, dma(3), dma(3),
             pltpu.SemaphoreType.DMA, pltpu.SemaphoreType.DMA,
-            dma(4, 4), dma(4, 4), dma(4), dma(4), dma(3), dma(3),
-            dma(8), dma(8), dma(7), dma(7),
+            dma(4, 4), dma(4, 4), dma(4), dma(4), dma(4), dma(4), dma(3), dma(3),
+            dma(8), dma(8), dma(2, 4), dma(2, 4),
             dma(2, 4), dma(2, 4), dma(4), dma(4), dma(4, 4), dma(4, 4),
             dma(2, 4, 4), dma(2, 4, 4), dma(8, 2), dma(2, 2), dma(2, 2), dma(2, 2),
             dma(2, 2), dma(3),

time: 89.1 us -> 86 us (0.965)
  Pallas kernels: 84.5 us -> 81.1 us
    pallas_call x1, Pallas kernels: 84.5 us -> 81.1 us  [shards(): pl.pallas_call(kernel, out_shape=jax.ShapeDtypeStruct((PANEL, PANEL), BF1...]
where the time goes in v3:
time: 86 us; the launch traced here: 85.5 us
  Pallas kernels  81.1 us (94%)
  other arithmetic  2.94 us (3%)
    pallas_call x1, Pallas kernels, shards(): pl.pallas_call(kernel, out_shape=jax.ShapeDtypeStruct((PANEL, PANEL), BF1...  81.1 us
    convert_element_type x1, other arithmetic, shards(): return ld.astype(F32)  2.15 us

profile of v3, /device:TPU:8, one launch (start us, length us, event | category | flops | bytes accessed | tf_op | source)
XLA Modules:
  0.0 85.5 jit_solution(5689182795946476402)
XLA Ops:
  0.7 0.7 select_convert_fusion
  1.4 0.1 fusion.4
  1.4 0.1 pad_maximum_fusion.1
  1.6 0.6 broadcast_in_dim.12.labs
  2.2 81.1 %shard_map.46 = bf16[512,512]{1,0:T(8,128)(2,1)} custom-call(bf16[672,512]{1,0:T(8,128)(2,1)} %dose.1, f32[3,8,384]{2,1,0:T(8,128)} %broadcast_in_dim.12.labs, s32[1]{0:T(128)} %copy.5.live, s32[8]{0:T(128)} %weights.1), custom_call_target="tpu_custom_call" | custom-call | tf_op jit(solution)/shard_map/pallas_call | solution.py:537
  83.4 2.1 %convert_element_type.7 = f32[512,512]{1,0:T(8,128)} convert(bf16[512,512]{1,0:T(8,128)(2,1)} %shard_map.46) | non-fusion elementwise | flops 262144 | bytes 1572864 | tf_op jit(solution)/shard_map/convert_element_type | solution.py:578
  (8 shorter events, 0.0 us)

commit v4 on v3

--- a/solution.py
+++ b/solution.py
@@ -241,6 +241,8 @@
             ).wait()
         for way in (0, 1):
             z_start(1, way, slot)
+
+    def send_ring(slot):
         for way in (0, 1):
             ring_copy(way, slot).start()
             drains.append(ring_copy(way, slot))
@@ -269,15 +271,26 @@
     send_slices(0)
     send_row_sums()
     send_surplus()
+    send_slot(0)
+    for slot in (1, 2, 3):
+        fill_slot(slot)
+    send_labels()
+    send_ring(0)
+    for slot in (1, 2, 3):
+        send_slot(slot)
+        send_ring(slot)
     for source in range(4):
         pltpu.make_async_copy(slice_sums.at[0], row_sums.at[source], rowsum_recv.at[source]).wait()
     sums[...] = row_sums[0] + row_sums[1] + row_sums[2] + row_sums[3]
     for copy in sum_copies:
         copy.start()
         drains.append(copy)
-    send_slot(0)
-    send_labels()
-    fill_slot(1)
+    z_pass(1, 0)
+    z_pass(1, 1)
+    pass_ring(0)
+    z_pass(1, 2)
+    pass_ring(1)
+    z_pass(1, 3)
 
     for copy in sum_copies:
         copy.wait_recv()
@@ -330,35 +343,23 @@
     for way in (0, 1):
         ztab_start(1, way)
 
-    pass_ring(0)
-    z_pass(1, 0)
-    fill_slot(2)
-    send_slot(1)
-    ztab_pass(1)
-    fill_slot(3)
-    send_slot(2)
     z_pass(2, 0)
-    pass_ring(1)
-    z_pass(1, 1)
-    pass_far(0)
-    send_slot(3)
+    pass_ring(2)
+    z_pass(2, 1)
+    pass_ring(3)
     for source in range(4):
         pltpu.make_async_copy(own_lab, row_labs.at[source], lab_recv.at[source]).wait()
     for source in range(4):
         hot = jnp.where(row_labs[source] == cohorts, 1.0, 0.0).astype(F32)
         hots = jnp.concatenate([hot, hot, hot, jnp.zeros_like(hot)], axis=0)
         hot_ref[source] = hots.T.astype(BF16)
-    ztab_pass(2)
-    z_pass(1, 2)
-    pass_ring(2)
+    pass_far(0)
+    z_pass(2, 2)
     pass_far(1)
-    z_pass(2, 1)
-    z_pass(3, 0)
-    z_pass(1, 3)
-    pass_ring(3)
-    ztab_pass(3)
-    for slot in (2, 3):
-        pass_far(slot)
+    pass_far(2)
+    pass_far(3)
+    z_pass(2, 3)
+    ztab_pass(1)
 
     def packed(both):
         mean, multiplier = both[:COHORTS], both[COHORTS:]
@@ -377,7 +378,7 @@
     for d in range(4):
         for slot in range(4):
             core_copy(d, slot).wait_recv()
-    z_pass(2, 2)
+    z_pass(3, 0)
 
     def fill_panel(g, carry):
         table = packed(row_tab[g])
@@ -440,14 +441,15 @@
         s = plus(z, d, 8)
         make_partial(s, lambda source: z_raw[s, source], z_tab[s])
 
+    z_pass(3, 1)
+    z_pass(3, 2)
     make_partial(z, lambda source: raw[group, source], row_tab[group])
-    z_pass(2, 3)
-    z_pass(3, 1)
+    z_pass(3, 3)
+    ztab_pass(2)
     from_z(7)
     from_z(1)
     add_relay(z)
-    z_pass(3, 2)
-    z_pass(3, 3)
+    ztab_pass(3)
     from_z(6)
     add_relay(plus(z, 7, 8))
     from_z(2)
@@ -456,11 +458,11 @@
     add_relay(plus(z, 6, 8))
     from_z(3)
     add_relay(plus(z, 2, 8))
-    add_relay(plus(z, 5, 8))
     for slot in range(4):
         z_pass(4, slot)
     ztab_pass(4)
     from_z(4)
+    add_relay(plus(z, 5, 8))
     add_relay(plus(z, 3, 8))
     add_relay(plus(z, 4, 8))
 

time: 86 us -> 85.3 us (level)
  no operation moved by 1% of the time
where the time goes in v4:
time: 85.3 us; the launch traced here: 85 us
  Pallas kernels  80.6 us (94%)
  other arithmetic  2.94 us (3%)
    pallas_call x1, Pallas kernels, shards(): pl.pallas_call(kernel, out_shape=jax.ShapeDtypeStruct((PANEL, PANEL), BF1...  80.6 us
    convert_element_type x1, other arithmetic, shards(): return ld.astype(F32)  2.15 us

profile of v4, /device:TPU:8, one launch (start us, length us, event | category | flops | bytes accessed | tf_op | source)
XLA Modules:
  0.0 85.0 jit_solution(16830018705399035301)
XLA Ops:
  0.7 0.7 select_convert_fusion
  1.4 0.1 fusion.4
  1.4 0.1 pad_maximum_fusion.1
  1.6 0.6 broadcast_in_dim.12.labs
  2.2 80.6 %shard_map.46 = bf16[512,512]{1,0:T(8,128)(2,1)} custom-call(bf16[672,512]{1,0:T(8,128)(2,1)} %dose.1, f32[3,8,384]{2,1,0:T(8,128)} %broadcast_in_dim.12.labs, s32[1]{0:T(128)} %copy.5.live, s32[8]{0:T(128)} %weights.1), custom_call_target="tpu_custom_call" | custom-call | tf_op jit(solution)/shard_map/pallas_call | solution.py:539
  82.8 2.1 %convert_element_type.7 = f32[512,512]{1,0:T(8,128)} convert(bf16[512,512]{1,0:T(8,128)(2,1)} %shard_map.46) | non-fusion elementwise | flops 262144 | bytes 1572864 | tf_op jit(solution)/shard_map/convert_element_type | solution.py:580
  (8 shorter events, 0.0 us)

commit v5 on v4

--- a/solution.py
+++ b/solution.py
@@ -67,6 +67,194 @@
         pl.semaphore_signal(barrier, inc=1, device_id=peer, device_id_type=MESH)
 
     take_own.wait()
+    pl.semaphore_wait(barrier, len(peers))
+
+    drains = []
+
+    opposite = {"y": plus(y, 2, 4)}
+    onward = {"y": plus(y, 1 + 2 * core, 4)}
+
+    def sur_copy(b):
+        return remote(
+            dose.at[pl.ds((6 - b) * BLOCK, BLOCK)], surplus.at[b], sur_send.at[b], sur_recv.at[b], opposite
+        )
+
+    surlab_copy = remote(labs.at[1], surplus_lab, surlab_send, surlab_recv, opposite)
+
+    def send_surplus():
+        for b in range(3):
+            sur_copy(b).start()
+            drains.append(sur_copy(b))
+            if b == 0:
+                surlab_copy.start()
+                drains.append(surlab_copy)
+
+    group = 4 * core + x
+    mine = 2 * xl + core
+
+    def band(slot):
+        return pl.ds(slot * BLOCK, BLOCK)
+
+    def slice_copy(slot, d):
+        target = plus(x, d, 4)
+        if slot == 0:
+            src = own.at[band(0), pl.ds(pl.multiple_of(target * LANES, LANES), LANES)]
+        else:
+            src = cols.at[target, band(slot)]
+        dst = raw.at[4 * xh + target, mine, band(slot)]
+        return remote(src, dst, slice_send.at[slot, d], slice_recv.at[slot, mine], at_x(target, xh))
+
+    def slice_local(slot):
+        if slot == 0:
+            src = own.at[band(0), pl.ds(pl.multiple_of(x * LANES, LANES), LANES)]
+        else:
+            src = cols.at[x, band(slot)]
+        return pltpu.make_async_copy(src, raw.at[group, mine, band(slot)], slice_recv.at[slot, mine])
+
+    def lab_copy(d):
+        target = plus(x, d, 4)
+        return remote(
+            own_lab, row_labs.at[mine], lab_send.at[d], lab_recv.at[mine], at_x(target, xh)
+        )
+
+    def rowsum_copy(d):
+        target = plus(x, d, 4)
+        return remote(
+            slice_sums.at[target], row_sums.at[mine], rowsum_send.at[d], rowsum_recv.at[mine], at_x(target, xh)
+        )
+
+    def send_row_sums():
+        for d in (1, 2, 3):
+            rowsum_copy(d).start()
+            drains.append(rowsum_copy(d))
+
+        @pl.when(xh != core)
+        def _():
+            rowsum_copy(0).start()
+
+        @pl.when(xh == core)
+        def _():
+            pltpu.make_async_copy(slice_sums.at[x], row_sums.at[mine], rowsum_recv.at[mine]).start()
+
+    def send_slices(slot):
+        for d in (1, 2, 3):
+            slice_copy(slot, d).start()
+            drains.append(slice_copy(slot, d))
+
+        @pl.when(xh != core)
+        def _():
+            slice_copy(slot, 0).start()
+
+        @pl.when(xh == core)
+        def _():
+            slice_local(slot).start()
+
+    def send_labels():
+        surlab_copy.wait_recv()
+        own_lab[...] = jnp.maximum(labs[0], surplus_lab[...])
+        for d in (1, 2, 3):
+            lab_copy(d).start()
+            drains.append(lab_copy(d))
+
+        @pl.when(xh != core)
+        def _():
+            lab_copy(0).start()
+
+        @pl.when(xh == core)
+        def _():
+            pltpu.make_async_copy(own_lab, row_labs.at[mine], lab_recv.at[mine]).start()
+
+    def fill_slot(slot):
+        sur_copy(slot - 1).wait_recv()
+        block = jnp.where(slot < live[0], own[slot * BLOCK : (slot + 1) * BLOCK, :], surplus[slot - 1])
+        for s in range(4):
+            cols[s, slot * BLOCK : (slot + 1) * BLOCK, :] = block[:, s * LANES : (s + 1) * LANES]
+        send_slices(slot)
+
+    def z_copy(step, way, slot):
+        d = (9 - step) if way == 0 else (step - 1)
+        at = plus(z, d, 8)
+        dst = z_raw.at[at, :, band(slot)]
+        src = raw.at[group, :, band(slot)] if step == 1 else dst
+        return remote(
+            src, dst, z_send.at[way, step - 1, slot], z_recv.at[way, step - 1, slot],
+            {"z": plus(z, 1 if way == 0 else 7, 8)},
+        )
+
+    def goes(step, way, slot):
+        return step < 4 or (slot < 2) == (way == 0)
+
+    def z_start(step, way, slot):
+        if goes(step, way, slot):
+            z_copy(step, way, slot).start()
+            drains.append(z_copy(step, way, slot))
+
+    def z_pass(step, slot):
+        for way in (0, 1):
+            if goes(step, way, slot):
+                z_copy(step, way, slot).wait_recv()
+                if step < 4:
+                    z_start(step + 1, way, slot)
+
+    right, left = plus(x, 1, 4), plus(x, 3, 4)
+
+    def ring_copy(way, slot):
+        ref = raw.at[group, :, band(slot)]
+        return remote(
+            ref, ref, ring_send.at[way, slot], ring_recv.at[way, slot],
+            at_x(right if way == 0 else left, core),
+        )
+
+    def fwd_copy(slot):
+        who, to = (left, right) if slot < 2 else (right, left)
+        ref = raw.at[4 * core + who, :, band(slot)]
+        return remote(ref, ref, fwd_send.at[slot], fwd_recv.at[slot], at_x(to, core))
+
+    def core_copy(d, slot):
+        ref = raw.at[4 * core + plus(x, d, 4), :, band(slot)]
+        return remote(ref, ref, core_send.at[d, slot], core_recv.at[d, slot], {"co": 1 - core})
+
+    def core_start(d, slot):
+        core_copy(d, slot).start()
+        drains.append(core_copy(d, slot))
+
+    def send_slot(slot):
+        for source in range(4):
+            pltpu.make_async_copy(
+                cols.at[0, band(slot)], raw.at[group, source, band(slot)], slice_recv.at[slot, source]
+            ).wait()
+        for way in (0, 1):
+            z_start(1, way, slot)
+
+    def send_ring(slot):
+        for way in (0, 1):
+            ring_copy(way, slot).start()
+            drains.append(ring_copy(way, slot))
+        core_start(0, slot)
+
+    def pass_ring(slot):
+        ring_copy(0, slot).wait_recv()
+        if slot < 2:
+            fwd_copy(slot).start()
+        core_start(3, slot)
+        ring_copy(1, slot).wait_recv()
+        if slot >= 2:
+            fwd_copy(slot).start()
+        core_start(1, slot)
+        drains.append(fwd_copy(slot))
+
+    def pass_far(slot):
+        fwd_copy(slot).wait_recv()
+        core_start(2, slot)
+
+    sum_copies = [
+        remote(sums, far_sums.at[d - 1], sum_send.at[d - 1], sum_recv.at[d - 1], {"y": plus(y, d, 4)})
+        for d in (1, 2, 3)
+    ]
+
+    send_slices(0)
+    send_surplus()
+
     cohorts = lax.broadcasted_iota(jnp.int32, (COHORTS, ROWS), 0).astype(F32)
     totals = None
     for first, count, labels in ((0, ROWS, labs[0]), (ROWS, SURPLUS, labs[2])):
@@ -83,194 +271,7 @@
         totals = part if totals is None else totals + part
     for s in range(4):
         slice_sums[s] = totals[:, s * LANES : (s + 1) * LANES]
-    pl.semaphore_wait(barrier, len(peers))
-
-    drains = []
-
-    opposite = {"y": plus(y, 2, 4)}
-    onward = {"y": plus(y, 1 + 2 * core, 4)}
-
-    def sur_copy(b):
-        return remote(
-            dose.at[pl.ds((6 - b) * BLOCK, BLOCK)], surplus.at[b], sur_send.at[b], sur_recv.at[b], opposite
-        )
-
-    surlab_copy = remote(labs.at[1], surplus_lab, surlab_send, surlab_recv, opposite)
-
-    def send_surplus():
-        for b in range(3):
-            sur_copy(b).start()
-            drains.append(sur_copy(b))
-            if b == 0:
-                surlab_copy.start()
-                drains.append(surlab_copy)
-
-    group = 4 * core + x
-    mine = 2 * xl + core
-
-    def band(slot):
-        return pl.ds(slot * BLOCK, BLOCK)
-
-    def slice_copy(slot, d):
-        target = plus(x, d, 4)
-        if slot == 0:
-            src = own.at[band(0), pl.ds(pl.multiple_of(target * LANES, LANES), LANES)]
-        else:
-            src = cols.at[target, band(slot)]
-        dst = raw.at[4 * xh + target, mine, band(slot)]
-        return remote(src, dst, slice_send.at[slot, d], slice_recv.at[slot, mine], at_x(target, xh))
-
-    def slice_local(slot):
-        if slot == 0:
-            src = own.at[band(0), pl.ds(pl.multiple_of(x * LANES, LANES), LANES)]
-        else:
-            src = cols.at[x, band(slot)]
-        return pltpu.make_async_copy(src, raw.at[group, mine, band(slot)], slice_recv.at[slot, mine])
-
-    def lab_copy(d):
-        target = plus(x, d, 4)
-        return remote(
-            own_lab, row_labs.at[mine], lab_send.at[d], lab_recv.at[mine], at_x(target, xh)
-        )
-
-    def rowsum_copy(d):
-        target = plus(x, d, 4)
-        return remote(
-            slice_sums.at[target], row_sums.at[mine], rowsum_send.at[d], rowsum_recv.at[mine], at_x(target, xh)
-        )
-
-    def send_row_sums():
-        for d in (1, 2, 3):
-            rowsum_copy(d).start()
-            drains.append(rowsum_copy(d))
-
-        @pl.when(xh != core)
-        def _():
-            rowsum_copy(0).start()
-
-        @pl.when(xh == core)
-        def _():
-            pltpu.make_async_copy(slice_sums.at[x], row_sums.at[mine], rowsum_recv.at[mine]).start()
-
-    def send_slices(slot):
-        for d in (1, 2, 3):
-            slice_copy(slot, d).start()
-            drains.append(slice_copy(slot, d))
-
-        @pl.when(xh != core)
-        def _():
-            slice_copy(slot, 0).start()
-
-        @pl.when(xh == core)
-        def _():
-            slice_local(slot).start()
-
-    def send_labels():
-        surlab_copy.wait_recv()
-        own_lab[...] = jnp.maximum(labs[0], surplus_lab[...])
-        for d in (1, 2, 3):
-            lab_copy(d).start()
-            drains.append(lab_copy(d))
-
-        @pl.when(xh != core)
-        def _():
-            lab_copy(0).start()
-
-        @pl.when(xh == core)
-        def _():
-            pltpu.make_async_copy(own_lab, row_labs.at[mine], lab_recv.at[mine]).start()
-
-    def fill_slot(slot):
-        sur_copy(slot - 1).wait_recv()
-        block = jnp.where(slot < live[0], own[slot * BLOCK : (slot + 1) * BLOCK, :], surplus[slot - 1])
-        for s in range(4):
-            cols[s, slot * BLOCK : (slot + 1) * BLOCK, :] = block[:, s * LANES : (s + 1) * LANES]
-        send_slices(slot)
-
-    def z_copy(step, way, slot):
-        d = (9 - step) if way == 0 else (step - 1)
-        at = plus(z, d, 8)
-        dst = z_raw.at[at, :, band(slot)]
-        src = raw.at[group, :, band(slot)] if step == 1 else dst
-        return remote(
-            src, dst, z_send.at[way, step - 1, slot], z_recv.at[way, step - 1, slot],
-            {"z": plus(z, 1 if way == 0 else 7, 8)},
-        )
-
-    def goes(step, way, slot):
-        return step < 4 or (slot < 2) == (way == 0)
-
-    def z_start(step, way, slot):
-        if goes(step, way, slot):
-            z_copy(step, way, slot).start()
-            drains.append(z_copy(step, way, slot))
-
-    def z_pass(step, slot):
-        for way in (0, 1):
-            if goes(step, way, slot):
-                z_copy(step, way, slot).wait_recv()
-                if step < 4:
-                    z_start(step + 1, way, slot)
-
-    right, left = plus(x, 1, 4), plus(x, 3, 4)
-
-    def ring_copy(way, slot):
-        ref = raw.at[group, :, band(slot)]
-        return remote(
-            ref, ref, ring_send.at[way, slot], ring_recv.at[way, slot],
-            at_x(right if way == 0 else left, core),
-        )
-
-    def fwd_copy(slot):
-        who, to = (left, right) if slot < 2 else (right, left)
-        ref = raw.at[4 * core + who, :, band(slot)]
-        return remote(ref, ref, fwd_send.at[slot], fwd_recv.at[slot], at_x(to, core))
-
-    def core_copy(d, slot):
-        ref = raw.at[4 * core + plus(x, d, 4), :, band(slot)]
-        return remote(ref, ref, core_send.at[d, slot], core_recv.at[d, slot], {"co": 1 - core})
-
-    def core_start(d, slot):
-        core_copy(d, slot).start()
-        drains.append(core_copy(d, slot))
-
-    def send_slot(slot):
-        for source in range(4):
-            pltpu.make_async_copy(
-                cols.at[0, band(slot)], raw.at[group, source, band(slot)], slice_recv.at[slot, source]
-            ).wait()
-        for way in (0, 1):
-            z_start(1, way, slot)
-
-    def send_ring(slot):
-        for way in (0, 1):
-            ring_copy(way, slot).start()
-            drains.append(ring_copy(way, slot))
-        core_start(0, slot)
-
-    def pass_ring(slot):
-        ring_copy(0, slot).wait_recv()
-        if slot < 2:
-            fwd_copy(slot).start()
-        core_start(3, slot)
-        ring_copy(1, slot).wait_recv()
-        if slot >= 2:
-            fwd_copy(slot).start()
-        core_start(1, slot)
-        drains.append(fwd_copy(slot))
-
-    def pass_far(slot):
-        fwd_copy(slot).wait_recv()
-        core_start(2, slot)
-
-    sum_copies = [
-        remote(sums, far_sums.at[d - 1], sum_send.at[d - 1], sum_recv.at[d - 1], {"y": plus(y, d, 4)})
-        for d in (1, 2, 3)
-    ]
-
-    send_slices(0)
     send_row_sums()
-    send_surplus()
     send_slot(0)
     for slot in (1, 2, 3):
         fill_slot(slot)
@@ -441,22 +442,22 @@
         s = plus(z, d, 8)
         make_partial(s, lambda source: z_raw[s, source], z_tab[s])
 
+    make_partial(z, lambda source: raw[group, source], row_tab[group])
     z_pass(3, 1)
+    from_z(7)
+    from_z(1)
     z_pass(3, 2)
-    make_partial(z, lambda source: raw[group, source], row_tab[group])
+    add_relay(z)
     z_pass(3, 3)
     ztab_pass(2)
-    from_z(7)
-    from_z(1)
-    add_relay(z)
-    ztab_pass(3)
     from_z(6)
     add_relay(plus(z, 7, 8))
     from_z(2)
     add_relay(plus(z, 1, 8))
+    ztab_pass(3)
     from_z(5)
+    from_z(3)
     add_relay(plus(z, 6, 8))
-    from_z(3)
     add_relay(plus(z, 2, 8))
     for slot in range(4):
         z_pass(4, slot)

time: 85.3 us -> 82.6 us (0.968)
  Pallas kernels: 80.6 us -> 78 us
    pallas_call x1, Pallas kernels: 80.6 us -> 78 us  [shards(): pl.pallas_call(kernel, out_shape=jax.ShapeDtypeStruct((PANEL, PANEL), BF1...]
where the time goes in v5:
time: 82.6 us; the launch traced here: 82.3 us
  Pallas kernels  78 us (94%)
  other arithmetic  2.94 us (4%)
    pallas_call x1, Pallas kernels, shards(): pl.pallas_call(kernel, out_shape=jax.ShapeDtypeStruct((PANEL, PANEL), BF1...  78 us
    convert_element_type x1, other arithmetic, shards(): return ld.astype(F32)  2.15 us

profile of v5, /device:TPU:8, one launch (start us, length us, event | category | flops | bytes accessed | tf_op | source)
XLA Modules:
  0.0 82.3 jit_solution(680199146521423024)
XLA Ops:
  0.7 0.7 select_convert_fusion
  1.4 0.1 fusion.4
  1.4 0.1 pad_maximum_fusion.1
  1.6 0.6 broadcast_in_dim.12.labs
  2.2 78.0 %shard_map.46 = bf16[512,512]{1,0:T(8,128)(2,1)} custom-call(bf16[672,512]{1,0:T(8,128)(2,1)} %dose.1, f32[3,8,384]{2,1,0:T(8,128)} %broadcast_in_dim.12.labs, s32[1]{0:T(128)} %copy.5.live, s32[8]{0:T(128)} %weights.1), custom_call_target="tpu_custom_call" | custom-call | tf_op jit(solution)/shard_map/pallas_call | solution.py:540
  80.2 2.1 %convert_element_type.7 = f32[512,512]{1,0:T(8,128)} convert(bf16[512,512]{1,0:T(8,128)(2,1)} %shard_map.46) | non-fusion elementwise | flops 262144 | bytes 1572864 | tf_op jit(solution)/shard_map/convert_element_type | solution.py:581
  (8 shorter events, 0.0 us)

commit v6 on v5

--- a/solution.py
+++ b/solution.py
@@ -447,22 +447,22 @@
     from_z(7)
     from_z(1)
     z_pass(3, 2)
+    ztab_pass(2)
+    z_pass(3, 3)
+    from_z(6)
+    from_z(2)
     add_relay(z)
-    z_pass(3, 3)
-    ztab_pass(2)
-    from_z(6)
-    add_relay(plus(z, 7, 8))
-    from_z(2)
-    add_relay(plus(z, 1, 8))
     ztab_pass(3)
     from_z(5)
+    add_relay(plus(z, 7, 8))
     from_z(3)
-    add_relay(plus(z, 6, 8))
-    add_relay(plus(z, 2, 8))
+    add_relay(plus(z, 1, 8))
     for slot in range(4):
         z_pass(4, slot)
     ztab_pass(4)
     from_z(4)
+    add_relay(plus(z, 6, 8))
+    add_relay(plus(z, 2, 8))
     add_relay(plus(z, 5, 8))
     add_relay(plus(z, 3, 8))
     add_relay(plus(z, 4, 8))

time: 82.6 us -> 79.9 us (0.967)
  Pallas kernels: 78 us -> 75.3 us
    pallas_call x1, Pallas kernels: 78 us -> 75.3 us  [shards(): pl.pallas_call(kernel, out_shape=jax.ShapeDtypeStruct((PANEL, PANEL), BF1...]
where the time goes in v6:
time: 79.9 us; the launch traced here: 79.7 us
  Pallas kernels  75.3 us (94%)
  other arithmetic  2.94 us (4%)
    pallas_call x1, Pallas kernels, shards(): pl.pallas_call(kernel, out_shape=jax.ShapeDtypeStruct((PANEL, PANEL), BF1...  75.3 us
    convert_element_type x1, other arithmetic, shards(): return ld.astype(F32)  2.15 us

profile of v6, /device:TPU:8, one launch (start us, length us, event | category | flops | bytes accessed | tf_op | source)
XLA Modules:
  0.0 79.7 jit_solution(2066521606575014682)
XLA Ops:
  0.7 0.7 select_convert_fusion
  1.4 0.1 fusion.4
  1.4 0.1 pad_maximum_fusion.1
  1.6 0.6 broadcast_in_dim.12.labs
  2.2 75.3 %shard_map.46 = bf16[512,512]{1,0:T(8,128)(2,1)} custom-call(bf16[672,512]{1,0:T(8,128)(2,1)} %dose.1, f32[3,8,384]{2,1,0:T(8,128)} %broadcast_in_dim.12.labs, s32[1]{0:T(128)} %copy.5.live, s32[8]{0:T(128)} %weights.1), custom_call_target="tpu_custom_call" | custom-call | tf_op jit(solution)/shard_map/pallas_call | solution.py:540
  77.5 2.1 %convert_element_type.7 = f32[512,512]{1,0:T(8,128)} convert(bf16[512,512]{1,0:T(8,128)(2,1)} %shard_map.46) | non-fusion elementwise | flops 262144 | bytes 1572864 | tf_op jit(solution)/shard_map/convert_element_type | solution.py:581
  (8 shorter events, 0.0 us)

commit v7 on v6

--- a/solution.py
+++ b/solution.py
@@ -457,11 +457,11 @@
     add_relay(plus(z, 7, 8))
     from_z(3)
     add_relay(plus(z, 1, 8))
+    add_relay(plus(z, 6, 8))
     for slot in range(4):
         z_pass(4, slot)
     ztab_pass(4)
     from_z(4)
-    add_relay(plus(z, 6, 8))
     add_relay(plus(z, 2, 8))
     add_relay(plus(z, 5, 8))
     add_relay(plus(z, 3, 8))

time: 79.9 us -> 79.9 us (level)
  no operation moved by 1% of the time
where the time goes in v7:
time: 79.9 us; the launch traced here: 79.7 us
  Pallas kernels  75.3 us (94%)
  other arithmetic  2.94 us (4%)
    pallas_call x1, Pallas kernels, shards(): pl.pallas_call(kernel, out_shape=jax.ShapeDtypeStruct((PANEL, PANEL), BF1...  75.3 us
    convert_element_type x1, other arithmetic, shards(): return ld.astype(F32)  2.15 us

profile of v7, /device:TPU:8, one launch (start us, length us, event | category | flops | bytes accessed | tf_op | source)
XLA Modules:
  0.0 79.7 jit_solution(12612989699231653677)
XLA Ops:
  0.7 0.7 select_convert_fusion
  1.4 0.1 fusion.4
  1.4 0.1 pad_maximum_fusion.1
  1.6 0.6 broadcast_in_dim.12.labs
  2.2 75.3 %shard_map.46 = bf16[512,512]{1,0:T(8,128)(2,1)} custom-call(bf16[672,512]{1,0:T(8,128)(2,1)} %dose.1, f32[3,8,384]{2,1,0:T(8,128)} %broadcast_in_dim.12.labs, s32[1]{0:T(128)} %copy.5.live, s32[8]{0:T(128)} %weights.1), custom_call_target="tpu_custom_call" | custom-call | tf_op jit(solution)/shard_map/pallas_call | solution.py:540
  77.5 2.1 %convert_element_type.7 = f32[512,512]{1,0:T(8,128)} convert(bf16[512,512]{1,0:T(8,128)(2,1)} %shard_map.46) | non-fusion elementwise | flops 262144 | bytes 1572864 | tf_op jit(solution)/shard_map/convert_element_type | solution.py:581
  (8 shorter events, 0.0 us)
